TPU v7x, 512 devices: a whole 4x8x8 slice. The times are simulated.
512 devices in a mesh: gx: 8 (over z_hi, core), gy: 8 (over y), gz: 8 (over x, z_lo).
Axes of the slice: x: 4, y: 8, z: 8 (z_hi: 4, z_lo: 2; z = z_hi * 2 + z_lo), core: 2. Of those that a mesh axis runs over, the one named last changes fastest.
Arguments:
- features: bfloat16 [8, 8, 8, 128, 128], P('gx', 'gy', 'gz'), may hold values from -6 to 6
- positions: float32 [8, 8, 8, 3, 128], P('gx', 'gy', 'gz'), may hold values from 0 to 1
- counts: int32 [8, 8, 8], P('gx', 'gy', 'gz'), may hold values from 1 to 128, as said below
- w_proj: bfloat16 [4, 128, 128], replicated, may hold values from -0.5 to 0.5
- w_mix: bfloat16 [128, 128], replicated, may hold values from -0.5 to 0.5
- w_long: bfloat16 [64, 128], replicated, may hold values from -0.75 to 0.75
- w_charge: bfloat16 [64, 128], replicated, may hold values from -0.5 to 0.5
- charge_bias: float32 [64], replicated, may hold values from -4 to 4
- w_energy: float32 [128], replicated, may hold values from -0.5 to 0.5
- k_filter: float32 [64, 2048], replicated, may hold values from 0.1 to 1
- k_index: int32 [3, 2048], replicated, may hold values from -6 to 6
Outputs:
- updated: bfloat16 [8, 8, 8, 128, 128], P('gx', 'gy', 'gz')
- energies: float32 [8, 8, 8, 128], P('gx', 'gy', 'gz')
- forces: float32 [8, 8, 8, 3, 128], P('gx', 'gy', 'gz')
Inputs may be any that keep to these rules, and one draw needn't show every extreme that they name: Slots 0 to counts[x,y,z] - 1 of cell (x,y,z) hold live atoms, the rest are padding; some cell holds 128 live atoms.
All inputs are finite; a program needn't handle non-finite values.
Results may differ from a plain program's by a relative error of at most 0.0068.
Values may be sent and summed in bfloat16 or wider, within the bound.
A program may use at most 64 MiB of HBM per device.

v0:
```python
import math

import jax
import jax.numpy as jnp
from jax import lax
from jax.sharding import PartitionSpec as P

CUTOFF = 0.9
GAMMAS = (1.0, 3.0, 8.0, 20.0)
PRECISE = lax.Precision.HIGHEST
CONTRACT_LAST = (((1,), (1,)), ((), ()))
CONTRACT_FIRST = (((0,), (0,)), ((), ()))


def extended(value, sides, width):
    for axis, dim in sides:
        peers, length = (lax.axis_size(axis), value.shape[dim])
        up = [(i, (i + 1) % peers) for i in range(peers)]
        down = [(j, i) for i, j in up]
        last = lax.slice_in_dim(value, length - width, length, axis=dim)
        initial = lax.slice_in_dim(value, 0, width, axis=dim)
        before = lax.ppermute(last, axis, up)
        after = lax.ppermute(initial, axis, down)
        value = jnp.concatenate([before, value, after], axis=dim)
    return value


def silu_grad(values):
    sigma = jax.nn.sigmoid(values)
    return sigma * (1.0 + values * (1.0 - sigma))


def pair_geometry(centre, others, neighbour):
    cell_shift = (
        jnp.stack([neighbour // 9, neighbour // 3 % 3, neighbour % 3]).astype(jnp.float32) - 1.0
    )
    offset_vec = others[:, None, :] + cell_shift[:, None, None] - centre[:, :, None]
    scaled = jnp.sum(offset_vec * offset_vec, axis=0) / (CUTOFF * CUTOFF)
    atom_count = centre.shape[1]
    slot_ids = jnp.arange(atom_count, dtype=jnp.int32)
    self_pair = (slot_ids[:, None] == slot_ids[None, :]) & (neighbour == 13)
    keep_mask = jnp.where(self_pair, 0.0, 1.0).astype(jnp.float32)
    envelope_base = jnp.maximum(1.0 - scaled, 0.0)
    decay_rates = jnp.asarray(GAMMAS, dtype=jnp.float32)[None, :, None]
    decay_terms = jnp.exp(-decay_rates * scaled[:, None, :]) * keep_mask[:, None, :]
    envelope = (envelope_base * envelope_base)[:, None, :]
    radial = decay_terms * envelope
    radial_slope = decay_terms * (-decay_rates * envelope - 2.0 * envelope_base[:, None, :])
    return (offset_vec, radial, radial_slope)


def phases(absolute, wave_vec, first_wave, wave_block):
    wave_part = wave_vec[:, first_wave : first_wave + wave_block]
    phase_angle = (
        absolute[0][:, None] * wave_part[0][None, :]
        + absolute[1][:, None] * wave_part[1][None, :]
        + absolute[2][:, None] * wave_part[2][None, :]
    )
    return (jnp.cos(phase_angle), jnp.sin(phase_angle))


def structure(weights_rows, absolute, wave_vec, wave_block):
    cosine_parts = []
    sine_parts = []
    for first_wave in range(0, wave_vec.shape[1], wave_block):
        cosine, sine_part = phases(absolute, wave_vec, first_wave, wave_block)
        cosine_parts.append(jnp.dot(weights_rows, cosine, precision=PRECISE))
        sine_parts.append(jnp.dot(weights_rows, sine_part, precision=PRECISE))
    return (jnp.concatenate(cosine_parts, axis=1), jnp.concatenate(sine_parts, axis=1))


def shards(
    features,
    positions,
    counts,
    w_proj,
    w_mix,
    w_long,
    w_charge,
    charge_bias,
    w_energy,
    k_filter,
    k_index,
):
    own_rows = features[0, 0, 0]
    centre = positions[0, 0, 0]
    atom_count, channels = own_rows.shape
    basis_count = w_proj.shape[0]
    waves = k_index.shape[1]
    wave_block = min(512, waves)
    grid_sizes = (lax.axis_size("gx"), lax.axis_size("gy"), lax.axis_size("gz"))
    scale_long = 4.0 / math.sqrt(atom_count * grid_sizes[0] * grid_sizes[1] * grid_sizes[2] * waves)
    cell_anchor = jnp.stack(
        [lax.axis_index("gx"), lax.axis_index("gy"), lax.axis_index("gz")]
    ).astype(jnp.float32)
    living = (jnp.arange(atom_count, dtype=jnp.int32) < counts[0, 0, 0]).astype(jnp.float32)
    masked = own_rows * living[:, None].astype(jnp.bfloat16)
    extent = jnp.asarray(grid_sizes, dtype=jnp.float32)
    wave_vec = 2.0 * math.pi * k_index.astype(jnp.float32) / extent[:, None]
    absolute = centre + cell_anchor[:, None]
    charges = (
        jax.nn.silu(
            lax.dot_general(w_charge, masked, CONTRACT_LAST, preferred_element_type=jnp.float32)
            + charge_bias[:, None]
        )
        * living[None, :]
    )
    stacked_rows = jnp.concatenate([charges, living[None, :]], axis=0)
    local_c, local_s = structure(stacked_rows, absolute, wave_vec, wave_block)
    totals = lax.psum(
        (local_c, local_s, jnp.sum(charges, axis=1), jnp.sum(living)), ("gx", "gy", "gz")
    )
    charge_mean = totals[2] / totals[3]
    neutral = (charges - charge_mean[:, None]) * living[None, :]
    row_count = charges.shape[0]
    struct_c = totals[0][:row_count] - charge_mean[:, None] * totals[0][row_count:]
    struct_s = totals[1][:row_count] - charge_mean[:, None] * totals[1][row_count:]
    near_pos = extended(positions, (("gx", 0), ("gy", 1), ("gz", 2)), 1).reshape(27, 3, atom_count)
    local_proj = jnp.einsum(
        "jc,bcd->bjd", masked, w_proj, preferred_element_type=jnp.float32
    ).astype(jnp.bfloat16)
    near_feat = extended(masked[None, None, None], (("gx", 0), ("gy", 1), ("gz", 2)), 1).reshape(
        27, atom_count, channels
    )

    def fetch_basis(neighbour):
        near_rows = lax.dynamic_index_in_dim(near_feat, neighbour, 0, keepdims=False)
        return (
            jnp.einsum("jc,bcd->bjd", near_rows, w_proj, preferred_element_type=jnp.float32)
            .astype(jnp.bfloat16)
            .reshape(basis_count * atom_count, channels)
        )

    def add_message(neighbour, message):
        others = lax.dynamic_index_in_dim(near_pos, neighbour, 0, keepdims=False)
        offset_vec, radial, radial_slope = pair_geometry(centre, others, neighbour)
        return message + jnp.dot(
            radial.astype(jnp.bfloat16).reshape(atom_count, -1),
            fetch_basis(neighbour),
            preferred_element_type=jnp.float32,
        )

    message = lax.fori_loop(0, 27, add_message, jnp.zeros((atom_count, channels), jnp.float32))
    filtered_cos = k_filter * struct_c
    filtered_sin = k_filter * struct_s
    potential = jnp.zeros(charges.shape, jnp.float32)
    for first_wave in range(0, waves, wave_block):
        cosine, sine_part = phases(absolute, wave_vec, first_wave, wave_block)
        potential = (
            potential
            + lax.dot_general(
                filtered_cos[:, first_wave : first_wave + wave_block],
                cosine,
                CONTRACT_LAST,
                precision=PRECISE,
            )
            + lax.dot_general(
                filtered_sin[:, first_wave : first_wave + wave_block],
                sine_part,
                CONTRACT_LAST,
                precision=PRECISE,
            )
        )
    potential = scale_long * potential
    pre_act = jnp.dot(
        message.astype(jnp.bfloat16), w_mix, preferred_element_type=jnp.float32
    ) + lax.dot_general(
        potential.astype(jnp.bfloat16), w_long, CONTRACT_FIRST, preferred_element_type=jnp.float32
    )
    refined = own_rows.astype(jnp.float32) + jax.nn.silu(pre_act)
    energy = living * jnp.sum(jax.nn.silu(refined) * w_energy[None, :], axis=1)
    grad_new = living[:, None] * w_energy[None, :] * silu_grad(refined)
    grad_pre = (grad_new * silu_grad(pre_act)).astype(jnp.bfloat16)
    adjoint = lax.dot_general(
        grad_pre, w_mix, CONTRACT_LAST, preferred_element_type=jnp.float32
    ).astype(jnp.bfloat16)
    pull_back = lax.dot_general(w_long, grad_pre, CONTRACT_LAST, preferred_element_type=jnp.float32)
    near_adjoint = extended(
        adjoint[None, None, None], (("gx", 0), ("gy", 1), ("gz", 2)), 1
    ).reshape(27, atom_count, channels)
    pull_c, pull_s = structure(pull_back, absolute, wave_vec, wave_block)
    back_c, back_s = lax.psum((pull_c, pull_s), ("gx", "gy", "gz"))

    def add_force(neighbour, near_force):
        others = lax.dynamic_index_in_dim(near_pos, neighbour, 0, keepdims=False)
        offset_vec, radial, radial_slope = pair_geometry(centre, others, neighbour)
        first_term = lax.dot_general(
            adjoint, fetch_basis(neighbour), CONTRACT_LAST, preferred_element_type=jnp.float32
        ).reshape(atom_count, basis_count, atom_count)
        near_rows = lax.dynamic_index_in_dim(near_adjoint, neighbour, 0, keepdims=False)
        second_term = jnp.einsum(
            "bic,jc->ibj", local_proj, near_rows, preferred_element_type=jnp.float32
        )
        strength = jnp.sum(radial_slope * (first_term + second_term), axis=1)
        return near_force + 2.0 / (CUTOFF * CUTOFF) * jnp.sum(
            strength[None, :, :] * offset_vec, axis=2
        )

    near_force = lax.fori_loop(0, 27, add_force, jnp.zeros((3, atom_count), jnp.float32))
    mixing = jnp.concatenate([pull_back, neutral], axis=0)
    weights_along = jnp.concatenate([filtered_sin, k_filter * back_s], axis=0)
    weights_across = jnp.concatenate([filtered_cos, k_filter * back_c], axis=0)
    ewald_grad = jnp.zeros((3, atom_count), jnp.float32)
    for first_wave in range(0, waves, wave_block):
        cosine, sine_part = phases(absolute, wave_vec, first_wave, wave_block)
        along_term = lax.dot_general(
            mixing,
            weights_along[:, first_wave : first_wave + wave_block],
            CONTRACT_FIRST,
            precision=PRECISE,
        )
        across_term = lax.dot_general(
            mixing,
            weights_across[:, first_wave : first_wave + wave_block],
            CONTRACT_FIRST,
            precision=PRECISE,
        )
        ewald_grad = ewald_grad + lax.dot_general(
            wave_vec[:, first_wave : first_wave + wave_block],
            cosine * along_term - sine_part * across_term,
            CONTRACT_LAST,
            precision=PRECISE,
        )
    forces = near_force - scale_long * ewald_grad
    return (
        refined.astype(jnp.bfloat16)[None, None, None],
        energy[None, None, None],
        forces[None, None, None],
    )


def solution(mesh):
    in_specs = (
        P("gx", "gy", "gz", None, None),
        P("gx", "gy", "gz", None, None),
        P("gx", "gy", "gz"),
        P(),
        P(),
        P(),
        P(),
        P(),
        P(),
        P(),
        P(),
    )
    out_specs = (
        P("gx", "gy", "gz", None, None),
        P("gx", "gy", "gz", None),
        P("gx", "gy", "gz", None, None),
    )
    return jax.shard_map(shards, mesh=mesh, in_specs=in_specs, out_specs=out_specs, check_vma=False)
```

profile of v0, /device:TPU:1, one launch (start us, length us, event | category | flops | bytes accessed | tf_op | source)
XLA Modules:
  0.0 663.1 jit_solution(11404104133226041706)
XLA Ops:
  7.2 7.2 %collective-permute-start = (f32[1,1,1,3,128]{4,2,3,1,0:T(1,128)}, f32[1,1,1,3,128]{4,2,3,1,0:T(1,128)S(1)}, u32[]{:S(2)}, u32[]{:S(2)}) collective-permute-start(f32[1,1,1,3,128]{4,2,3,1,0:T(1,128)} %param.19), channel_id=1, source_target_pairs={{0,64},{64,128},{128,192},{192,256},{256,320},{320,384},{384,448},... | collective-permute-start | bytes 4616 | tf_op jit(solution)/shard_map/ppermute | solution.py:22
  14.4 3.5 collective-permute-start.1
  19.5 5.8 collective-permute-start.7
  25.3 1.9 collective-permute-start.6
  41.5 101.2 %all-reduce = (f32[64]{0:T(128)S(1)}, f32[]{:T(128)}) all-reduce(f32[64]{0:T(128)S(1)} %get-tuple-element.752, f32[]{:T(128)} %fusion.291), channel_id=1, replica_groups=mesh['gx'=8,'gy'=8,'gz'=8] {'gx','gy','gz'}, use_global_device_ids=true, to_apply=%region_5.6 | all-reduce | flops 65 | bytes 520 | tf_op jit(solution)/shard_map/psum | solution.py:110
  143.3 2.6 collective-permute-start.3
  145.9 2.7 collective-permute-start.2
  148.7 3.8 collective-permute-start.9
  152.4 1.9 collective-permute-start.8
  154.4 2.5 collective-permute-start.5
  156.9 2.8 collective-permute-start.4
  159.8 4.6 collective-permute-start.11
  164.4 2.1 collective-permute-start.10
  166.7 2.0 collective-permute-done.11
  168.7 8.2 %collective-permute-done.10 = bf16[3,3,1,128,128]{4,3,2,1,0:T(8,128)(2,1)S(1)} collective-permute-done((bf16[3,3,1,128,128]{4,3,2,1,0:T(8,128)(2,1)S(1)}, bf16[3,3,1,128,128]{4,3,2,1,0:T(8,128)(2,1)S(1)}, u32[]{:S(2)}, u32[]{:S(2)}) %collective-permute-start.10) | collective-permute-done | bytes 294944 | tf_op jit(solution)/shard_map/ppermute | solution.py:22
  177.7 20.3 %while.36 = (s32[]{:T(128)}, f32[128,128]{1,0:T(8,128)S(1)}, f32[27,3,128]{2,1,0:T(4,128)S(1)}, f32[1,1,1,3,128]{4,3,2,1,0:T(4,128)S(1)}, bf16[27,128,128]{2,1,0...) while((s32[]{:T(128)}, f32[128,128]{1,0:T(8,128)S(1)}, ...), condition=%wide.region_2.3_spmd.clone.clone, body=%wide.region_0.0_spmd.clone.clone.sunk | while | flops 34161064 | bytes 826287 | solution.py:143
  198.2 119.0 %all-reduce.8.cloned.1.call-done = (f32[65,2048]{1,0:T(8,128)}, f32[65,2048]{1,0:T(8,128)}) async-done(((f32[65,2048]{1,0:T(8,128)}, f32[65,2048]{1,0:T(8,128)}), (f32[65,2048]{1,0:T(8,128)}, f32[65,2048]{1,0:T(8,128)})) %all-reduce.8.cloned.1.call-update) | async-done | bytes 1064976 | tf_op jit(solution)/shard_map/psum | solution.py:110
  319.0 1.4 fusion.48
  323.0 1.3 convolution_add_fusion.7
  325.6 1.3 convolution_add_fusion.5
  328.2 1.3 convolution_add_fusion.3
  331.9 2.3 collective-permute-start.13
  334.2 4.4 collective-permute-start.12
  348.3 3.3 collective-permute-start.15
  351.6 2.0 collective-permute-start.14
  354.8 3.8 collective-permute-done.14
  359.4 4.7 collective-permute-start.17
  364.1 2.2 collective-permute-start.16
  370.0 7.4 %collective-permute-done.16 = bf16[3,3,1,128,128]{4,3,2,1,0:T(8,128)(2,1)} collective-permute-done((bf16[3,3,1,128,128]{4,3,2,1,0:T(8,128)(2,1)}, bf16[3,3,1,128,128]{4,3,2,1,0:T(8,128)(2,1)}, u32[]{:S(2)}, u32[]{:S(2)}) %collective-permute-start.16) | collective-permute-done | bytes 294944 | tf_op jit(solution)/shard_map/ppermute | solution.py:22
  377.4 2.0 pad_maximum_fusion.1
  379.4 67.3 %while.37 = (s32[]{:T(128)}, f32[3,128]{1,0:T(4,128)S(1)}, f32[27,3,128]{2,1,0:T(4,128)S(1)}, f32[1,1,1,3,128]{4,3,2,1,0:T(4,128)S(1)}, bf16[27,128,128]{2,1,0:T...) while((s32[]{:T(128)}, f32[3,128]{1,0:T(4,128)S(1)}, ...), condition=%wide.region_14.15_spmd.clone.clone, body=%wide.region_10.14_spmd.clone.clone.sunk | while | flops 51315852 | bytes 2604507 | solution.py:199
  446.7 195.4 %all-reduce.6.cloned.1.call-done = (f32[64,2048]{1,0:T(8,128)}, f32[64,2048]{1,0:T(8,128)}) async-done(((f32[64,2048]{1,0:T(8,128)}, f32[64,2048]{1,0:T(8,128)}), (f32[64,2048]{1,0:T(8,128)}, f32[64,2048]{1,0:T(8,128)})) %all-reduce.6.cloned.1.call-update) | async-done | bytes 1048592 | tf_op jit(solution)/shard_map/psum | solution.py:182
  (715 shorter events, 134.7 us)
Async XLA Ops:
  7.2 310.1 %all-reduce.8.cloned.1.call-start = ((), (), s32[]{:S(2)}) async-start(), calls=%async_computation.1 | async-start | bytes 2359296 | tf_op jit(solution)/shard_map/psum | solution.py:110
  7.2 136.0 %collective-permute-start = (f32[1,1,1,3,128]{4,2,3,1,0:T(1,128)}, f32[1,1,1,3,128]{4,2,3,1,0:T(1,128)S(1)}, u32[]{:S(2)}, u32[]{:S(2)}) collective-permute-start(f32[1,1,1,3,128]{4,2,3,1,0:T(1,128)} %param.19), channel_id=1, source_target_pairs={{0,64},{64,128},{128,192},{192,256},{256,320},{320,384},{384,448},... | collective-permute-start | bytes 4616 | tf_op jit(solution)/shard_map/ppermute | solution.py:22
  14.4 128.9 %collective-permute-start.1 = (f32[1,1,1,3,128]{4,2,3,1,0:T(1,128)}, f32[1,1,1,3,128]{4,2,3,1,0:T(1,128)S(1)}, u32[]{:S(2)}, u32[]{:S(2)}) collective-permute-start(f32[1,1,1,3,128]{4,2,3,1,0:T(1,128)} %param.19), channel_id=1, source_target_pairs={{64,0},{128,64},{192,128},{256,192},{320,256},{384,320},{448,384},... | collective-permute-start | bytes 4616 | tf_op jit(solution)/shard_map/ppermute | solution.py:23
  19.5 129.1 %collective-permute-start.7 = (bf16[1,1,1,128,128]{4,3,2,1,0:T(8,128)(2,1)S(1)}, bf16[1,1,1,128,128]{4,3,2,1,0:T(8,128)(2,1)S(1)}, u32[]{:S(2)}, u32[]{:S(2)}) collective-permute-start(bf16[1,1,1,128,128]{4,3,2,1,0:T(8,128)(2,1)S(1)} %broadcast_multiply_fusion.2), channel_id=1, source_target_pairs={{64,0},{128,64},{192,128},{256,192},{320,256},{384,320},{448,384},... | collective-permute-start | bytes 98312 | tf_op jit(solution)/shard_map/ppermute | solution.py:23
  25.3 123.4 %collective-permute-start.6 = (bf16[1,1,1,128,128]{4,3,2,1,0:T(8,128)(2,1)S(1)}, bf16[1,1,1,128,128]{4,3,2,1,0:T(8,128)(2,1)S(1)}, u32[]{:S(2)}, u32[]{:S(2)}) collective-permute-start(bf16[1,1,1,128,128]{4,3,2,1,0:T(8,128)(2,1)S(1)} %broadcast_multiply_fusion.2), channel_id=1, source_target_pairs={{0,64},{64,128},{128,192},{192,256},{256,320},{320,384},{384,448},... | collective-permute-start | bytes 98312 | tf_op jit(solution)/shard_map/ppermute | solution.py:22
  27.4 315.0 %copy-start.26 = (f32[1,512]{1,0:T(1,128)}, f32[1,512]{1,0:T(1,128)S(1)}, u32[]{:S(2)}) copy-start(f32[1,512]{1,0:T(1,128)S(1)} %get-tuple-element.737) | copy-start | bytes 6148
  27.4 315.0 %copy-start.29 = (f32[1,512]{1,0:T(1,128)}, f32[1,512]{1,0:T(1,128)S(1)}, u32[]{:S(2)}) copy-start(f32[1,512]{1,0:T(1,128)S(1)} %get-tuple-element.747) | copy-start | bytes 6148
  27.4 316.2 %copy-start.8 = (f32[1,512]{1,0:T(1,128)}, f32[1,512]{1,0:T(1,128)S(1)}, u32[]{:S(2)}) copy-start(f32[1,512]{1,0:T(1,128)S(1)} %get-tuple-element.738) | copy-start | bytes 6148
  27.4 316.2 %copy-start.10 = (f32[1,512]{1,0:T(1,128)}, f32[1,512]{1,0:T(1,128)S(1)}, u32[]{:S(2)}) copy-start(f32[1,512]{1,0:T(1,128)S(1)} %get-tuple-element.739) | copy-start | bytes 6148
  27.4 316.2 %copy-start.12 = (f32[1,512]{1,0:T(1,128)}, f32[1,512]{1,0:T(1,128)S(1)}, u32[]{:S(2)}) copy-start(f32[1,512]{1,0:T(1,128)S(1)} %get-tuple-element.740) | copy-start | bytes 6148
  27.4 317.4 %copy-start.14 = (f32[1,512]{1,0:T(1,128)}, f32[1,512]{1,0:T(1,128)S(1)}, u32[]{:S(2)}) copy-start(f32[1,512]{1,0:T(1,128)S(1)} %get-tuple-element.741) | copy-start | bytes 6148
  27.5 317.4 %copy-start.16 = (f32[1,512]{1,0:T(1,128)}, f32[1,512]{1,0:T(1,128)S(1)}, u32[]{:S(2)}) copy-start(f32[1,512]{1,0:T(1,128)S(1)} %get-tuple-element.742) | copy-start | bytes 6148
  27.5 317.4 %copy-start.18 = (f32[1,512]{1,0:T(1,128)}, f32[1,512]{1,0:T(1,128)S(1)}, u32[]{:S(2)}) copy-start(f32[1,512]{1,0:T(1,128)S(1)} %get-tuple-element.743) | copy-start | bytes 6148
  27.5 319.5 %copy-start.20 = (f32[1,512]{1,0:T(1,128)}, f32[1,512]{1,0:T(1,128)S(1)}, u32[]{:S(2)}) copy-start(f32[1,512]{1,0:T(1,128)S(1)} %get-tuple-element.744) | copy-start | bytes 6148
  27.5 319.5 %copy-start.22 = (f32[1,512]{1,0:T(1,128)}, f32[1,512]{1,0:T(1,128)S(1)}, u32[]{:S(2)}) copy-start(f32[1,512]{1,0:T(1,128)S(1)} %get-tuple-element.745) | copy-start | bytes 6148
  27.5 319.5 %copy-start.24 = (f32[1,512]{1,0:T(1,128)}, f32[1,512]{1,0:T(1,128)S(1)}, u32[]{:S(2)}) copy-start(f32[1,512]{1,0:T(1,128)S(1)} %get-tuple-element.746) | copy-start | bytes 6148
  28.3 325.3 %copy-start.5 = (f32[128]{0:T(128)}, f32[128]{0:T(128)S(1)}, u32[]{:S(2)}) copy-start(f32[128]{0:T(128)S(1)} %get-tuple-element.751) | copy-start | bytes 1540
  40.4 601.8 %all-reduce.6.cloned.1.call-start = ((), (), s32[]{:S(2)}) async-start(), calls=%async_computation | async-start | bytes 2097152 | tf_op jit(solution)/shard_map/psum | solution.py:182
  143.3 11.1 %collective-permute-start.3 = (f32[3,1,1,3,128]{4,2,3,1,0:T(1,128)S(1)}, f32[3,1,1,3,128]{4,2,3,1,0:T(1,128)S(1)}, u32[]{:S(2)}, u32[]{:S(2)}) collective-permute-start(f32[3,1,1,3,128]{4,2,3,1,0:T(1,128)S(1)} %constant_dynamic-update-slice_fusion), channel_id=1, source_target_pairs={{8,0},{16,8},{24,16},{32,24},{40,32},{48,40},{56,48},{0,56},{9,1},... | collective-permute-start | bytes 13832 | tf_op jit(solution)/shard_map/ppermute | solution.py:23
  145.9 8.5 %collective-permute-start.2 = (f32[3,1,1,3,128]{4,2,3,1,0:T(1,128)S(1)}, f32[3,1,1,3,128]{4,2,3,1,0:T(1,128)S(1)}, u32[]{:S(2)}, u32[]{:S(2)}) collective-permute-start(f32[3,1,1,3,128]{4,2,3,1,0:T(1,128)S(1)} %constant_dynamic-update-slice_fusion), channel_id=1, source_target_pairs={{0,8},{8,16},{16,24},{24,32},{32,40},{40,48},{48,56},{56,0},{1,9},... | collective-permute-start | bytes 13832 | tf_op jit(solution)/shard_map/ppermute | solution.py:22
  148.7 11.1 %collective-permute-start.9 = (bf16[3,1,1,128,128]{4,3,2,1,0:T(8,128)(2,1)S(1)}, bf16[3,1,1,128,128]{4,3,2,1,0:T(8,128)(2,1)S(1)}, u32[]{:S(2)}, u32[]{:S(2)}) collective-permute-start(bf16[3,1,1,128,128]{4,3,2,1,0:T(8,128)(2,1)S(1)} %pad_maximum_fusion.12), channel_id=1, source_target_pairs={{8,0},{16,8},{24,16},{32,24},{40,32},{48,40},{56,48},{0,56},{9,1},... | collective-permute-start | bytes 294920 | tf_op jit(solution)/shard_map/ppermute | solution.py:23
  152.4 7.3 %collective-permute-start.8 = (bf16[3,1,1,128,128]{4,3,2,1,0:T(8,128)(2,1)S(1)}, bf16[3,1,1,128,128]{4,3,2,1,0:T(8,128)(2,1)S(1)}, u32[]{:S(2)}, u32[]{:S(2)}) collective-permute-start(bf16[3,1,1,128,128]{4,3,2,1,0:T(8,128)(2,1)S(1)} %pad_maximum_fusion.12), channel_id=1, source_target_pairs={{0,8},{8,16},{16,24},{24,32},{32,40},{40,48},{48,56},{56,0},{1,9},... | collective-permute-start | bytes 294920 | tf_op jit(solution)/shard_map/ppermute | solution.py:22
  154.4 12.2 %collective-permute-start.5 = (f32[3,3,1,3,128]{4,2,3,1,0:T(1,128)S(1)}, f32[3,3,1,3,128]{4,2,3,1,0:T(1,128)S(1)}, u32[]{:S(2)}, u32[]{:S(2)}) collective-permute-start(f32[3,3,1,3,128]{4,2,3,1,0:T(1,128)S(1)} %pad_maximum_fusion.17), channel_id=1, source_target_pairs={{1,0},{2,1},{3,2},{4,3},{5,4},{6,5},{7,6},{0,7},{9,8},{10,9},{11,1... | collective-permute-start | bytes 41480 | tf_op jit(solution)/shard_map/ppermute | solution.py:23
  156.9 9.7 %collective-permute-start.4 = (f32[3,3,1,3,128]{4,2,3,1,0:T(1,128)S(1)}, f32[3,3,1,3,128]{4,2,3,1,0:T(1,128)S(1)}, u32[]{:S(2)}, u32[]{:S(2)}) collective-permute-start(f32[3,3,1,3,128]{4,2,3,1,0:T(1,128)S(1)} %pad_maximum_fusion.17), channel_id=1, source_target_pairs={{0,1},{1,2},{2,3},{3,4},{4,5},{5,6},{6,7},{7,0},{8,9},{9,10},{10,1... | collective-permute-start | bytes 41480 | tf_op jit(solution)/shard_map/ppermute | solution.py:22
  159.8 8.9 %collective-permute-start.11 = (bf16[3,3,1,128,128]{4,3,2,1,0:T(8,128)(2,1)S(1)}, bf16[3,3,1,128,128]{4,3,2,1,0:T(8,128)(2,1)S(1)}, u32[]{:S(2)}, u32[]{:S(2)}) collective-permute-start(bf16[3,3,1,128,128]{4,3,2,1,0:T(8,128)(2,1)S(1)} %pad_maximum_fusion.6), channel_id=1, source_target_pairs={{1,0},{2,1},{3,2},{4,3},{5,4},{6,5},{7,6},{0,7},{9,8},{10,9},{11,1... | collective-permute-start | bytes 884744 | tf_op jit(solution)/shard_map/ppermute | solution.py:23
  164.4 12.5 %collective-permute-start.10 = (bf16[3,3,1,128,128]{4,3,2,1,0:T(8,128)(2,1)S(1)}, bf16[3,3,1,128,128]{4,3,2,1,0:T(8,128)(2,1)S(1)}, u32[]{:S(2)}, u32[]{:S(2)}) collective-permute-start(bf16[3,3,1,128,128]{4,3,2,1,0:T(8,128)(2,1)S(1)} %pad_maximum_fusion.6), channel_id=1, source_target_pairs={{0,1},{1,2},{2,3},{3,4},{4,5},{5,6},{6,7},{7,0},{8,9},{9,10},{10,1... | collective-permute-start | bytes 884744 | tf_op jit(solution)/shard_map/ppermute | solution.py:22
  331.9 16.4 %collective-permute-start.13 = (bf16[1,1,1,128,128]{4,3,2,1,0:T(8,128)(2,1)S(1)}, bf16[1,1,1,128,128]{4,3,2,1,0:T(8,128)(2,1)S(1)}, u32[]{:S(2)}, u32[]{:S(2)}) collective-permute-start(bf16[1,1,1,128,128]{4,3,2,1,0:T(8,128)(2,1)S(1)} %bitcast.201), channel_id=1, source_target_pairs={{64,0},{128,64},{192,128},{256,192},{320,256},{384,320},{448,384},... | collective-permute-start | bytes 98312 | tf_op jit(solution)/shard_map/ppermute | solution.py:23
  334.2 14.1 %collective-permute-start.12 = (bf16[1,1,1,128,128]{4,3,2,1,0:T(8,128)(2,1)S(1)}, bf16[1,1,1,128,128]{4,3,2,1,0:T(8,128)(2,1)S(1)}, u32[]{:S(2)}, u32[]{:S(2)}) collective-permute-start(bf16[1,1,1,128,128]{4,3,2,1,0:T(8,128)(2,1)S(1)} %bitcast.202), channel_id=1, source_target_pairs={{0,64},{64,128},{128,192},{192,256},{256,320},{320,384},{384,448},... | collective-permute-start | bytes 98312 | tf_op jit(solution)/shard_map/ppermute | solution.py:22
  348.3 6.6 collective-permute-start.15
  351.6 7.1 %collective-permute-start.14 = (bf16[3,1,1,128,128]{4,3,2,1,0:T(8,128)(2,1)S(1)}, bf16[3,1,1,128,128]{4,3,2,1,0:T(8,128)(2,1)S(1)}, u32[]{:S(2)}, u32[]{:S(2)}) collective-permute-start(bf16[3,1,1,128,128]{4,3,2,1,0:T(8,128)(2,1)S(1)} %pad_maximum_fusion.13), channel_id=1, source_target_pairs={{0,8},{8,16},{16,24},{24,32},{32,40},{40,48},{48,56},{56,0},{1,9},... | collective-permute-start | bytes 294920 | tf_op jit(solution)/shard_map/ppermute | solution.py:22
  359.4 10.6 %collective-permute-start.17 = (bf16[3,3,1,128,128]{4,3,2,1,0:T(8,128)(2,1)}, bf16[3,3,1,128,128]{4,3,2,1,0:T(8,128)(2,1)S(1)}, u32[]{:S(2)}, u32[]{:S(2)}) collective-permute-start(bf16[3,3,1,128,128]{4,3,2,1,0:T(8,128)(2,1)} %pad_maximum_fusion.7), channel_id=1, source_target_pairs={{1,0},{2,1},{3,2},{4,3},{5,4},{6,5},{7,6},{0,7},{9,8},{10,9},{11,1... | collective-permute-start | bytes 884744 | tf_op jit(solution)/shard_map/ppermute | solution.py:23
  364.1 13.3 %collective-permute-start.16 = (bf16[3,3,1,128,128]{4,3,2,1,0:T(8,128)(2,1)}, bf16[3,3,1,128,128]{4,3,2,1,0:T(8,128)(2,1)}, u32[]{:S(2)}, u32[]{:S(2)}) collective-permute-start(bf16[3,3,1,128,128]{4,3,2,1,0:T(8,128)(2,1)} %pad_maximum_fusion.7), channel_id=1, source_target_pairs={{0,1},{1,2},{2,3},{3,4},{4,5},{5,6},{6,7},{7,0},{8,9},{9,10},{10,1... | collective-permute-start | bytes 884744 | tf_op jit(solution)/shard_map/ppermute | solution.py:22
  (29 other events, 701.9 us)
Sparse Core Ops, SparseCore 0:
  40.5 276.7 all-reduce.7
  367.9 274.1 all-reduce.5
where the time goes:
time: 675 us; the launch traced here: 663 us
  waiting for transfers between devices  337 us (50%)
  blocking collectives  101 us (15%)
  matrix products  87.7 us (13%)
  starting transfers between devices  60.2 us (9%)
  other arithmetic  34.2 us (5%)
  local copies, waits for them, and re-layouts  18.9 us (3%)
  between operations  16.3 us (2%)
  loops' own time  7.66 us (1%)
    psum x1, waiting for transfers between devices, shards(): back_c, back_s = lax.psum((pull_c, pull_s), ('gx', 'gy', 'gz'))  195 us
    psum x1, waiting for transfers between devices, shards(): lax.psum((local_c, local_s, jnp.sum(charges, axis=1), jnp.sum(living)), (...  119 us
    psum x1, blocking collectives, shards(): lax.psum((local_c, local_s, jnp.sum(charges, axis=1), jnp.sum(living)), (...  101 us
    ppermute x9, starting transfers between devices, extended(): after = lax.ppermute(initial, axis, down)  33 us
    ppermute x9, starting transfers between devices, extended(): before = lax.ppermute(last, axis, up)  27.2 us
    dot_general x27, matrix products, add_force(): jnp.einsum('bic,jc->ibj', local_proj, near_rows, preferred_element_type=j...  26 us
    ppermute x9, waiting for transfers between devices, extended(): before = lax.ppermute(last, axis, up)  19.4 us
  transfers between devices with their start and end apart: 20, of which 7 were waited for; matrix products, arithmetic and copies ran while one was open for 16% of the time, Pallas kernels for 0%

commit v1 on v0

v1 whole, which is shorter than its diff:
```python
import functools
import math

import jax
import jax.numpy as jnp
from jax import lax
from jax.experimental import pallas as pl
from jax.experimental.pallas import tpu as pltpu
from jax.sharding import PartitionSpec as P

MESH = pl.DeviceIdType.MESH
CUTOFF2 = 0.9 * 0.9
ATOMS = 128
CHANNELS = 128
BASES = 4
EDGE = 8
WAVES = 2048
TOP = 6
SIDE = 2 * TOP + 1
TILES = 8
ROWS = 192
CHUNK = 24
SLOTS = TILES * ROWS
F32 = jnp.float32
BF16 = jnp.bfloat16
NT = (((1,), (1,)), ((), ()))
NN = (((1,), (0,)), ((), ()))
TN = (((0,), (0,)), ((), ()))


def dot(a, b, dims=NN):
    return lax.dot_general(a, b, dims, preferred_element_type=F32)


def split(value):
    high = value.astype(BF16)
    low = (value - high.astype(F32)).astype(BF16)
    return high, low


def dot3(a_high, a_low, b_high, b_low, dims=NN):
    return dot(a_high, b_high, dims) + dot(a_high, b_low, dims) + dot(a_low, b_high, dims)


def iota(shape, dim):
    return lax.broadcasted_iota(jnp.int32, shape, dim)


def sigmoid(v):
    return 1.0 / (1.0 + jnp.exp(-v))


def block_kernel(
    counts_ref,
    feat_ref,
    pos_ref,
    wproj_ref,
    wmix_ref,
    wlong_ref,
    wcharge_ref,
    rows_ref,
    kf_ref,
    kidx_ref,
    upd_ref,
    energy_ref,
    force_ref,
    nfeat,
    nadj,
    npos,
    trig,
    wave_f,
    wave_h,
    wave_l,
    filt,
    fs_h,
    fs_l,
    part1,
    got1z,
    mid1,
    got1y,
    low1,
    got1x,
    up1,
    all1,
    part2,
    got2z,
    mid2,
    got2y,
    low2,
    got2x,
    up2,
    all2,
    tot0,
    tot1,
    tot2,
    gott,
    pcol,
    rad,
    wcat,
    nbasis,
    acc,
    prod,
    uv,
    pull,
    send_sem,
    recv_sem,
    tsend,
    trecv,
    hsend,
    hrecv,
):
    me = tuple(lax.axis_index(name) for name in ("gx", "gy", "gz"))

    def device_at(axis, distance):
        coords = list(me)
        coords[axis] = lax.rem(me[axis] + distance, EDGE)
        return coords[axis], tuple(coords)

    barrier = pltpu.get_barrier_semaphore()
    for axis in range(3):
        for d in range(1, EDGE):
            pl.semaphore_signal(
                barrier, inc=1, device_id=device_at(axis, d)[1], device_id_type=MESH
            )

    sent = []

    def send(src, dst, ssem, rsem, device):
        copy = pltpu.make_async_remote_copy(
            src_ref=src,
            dst_ref=dst,
            send_sem=ssem,
            recv_sem=rsem,
            device_id=device,
            device_id_type=MESH,
        )
        copy.start()
        sent.append(copy)
        return copy

    def spread(axis, stage, source, target):
        copies = []
        for d in range(1, EDGE):
            peer, device = device_at(axis, d)
            copies.append(
                send(
                    source(peer),
                    target(d - 1),
                    send_sem.at[stage, d - 1],
                    recv_sem.at[stage, d - 1],
                    device,
                )
            )
        return copies

    def arrive(copies):
        for copy in copies:
            copy.wait_recv()

    live_row = (iota((1, ATOMS), 1) < counts_ref[0]).astype(F32)
    live_col = (iota((ATOMS, CHANNELS), 0) < counts_ref[0]).astype(F32)
    own = feat_ref[...]
    masked = own * live_col.astype(BF16)
    nfeat[13] = masked
    npos[13] = jnp.zeros((8, ATOMS), F32)
    npos[13, 0:3, :] = pos_ref[...]

    wcharge2 = jnp.concatenate([wcharge_ref[...], wcharge_ref[...]], axis=0)
    charge_pre = dot(masked, wcharge2, NT) + rows_ref[0:1, :]
    charge = charge_pre * sigmoid(charge_pre) * live_col
    tot0[0:1, :] = jnp.sum(charge, axis=0, keepdims=True)
    tot0[1:8, :] = jnp.broadcast_to(jnp.sum(live_col, axis=0, keepdims=True), (7, ATOMS))

    steps = iota((8, ATOMS), 0).astype(F32)
    for axis in range(3):
        unit = (pos_ref[axis : axis + 1, :] + me[axis].astype(F32)) * (1.0 / EDGE)
        orders = steps if axis < 2 else jnp.where(steps > 6.5, 0.0, steps)
        turns = orders * unit
        angle = (turns - jnp.floor(turns + 0.5)) * (2.0 * math.pi)
        trig[2 * axis] = jnp.cos(angle)
        trig[2 * axis + 1] = jnp.sin(angle)
    z_c = trig[4]
    z_s = trig[5]
    y_c = [jnp.broadcast_to(trig[2, m : m + 1, :], (8, ATOMS)) for m in range(TOP + 1)]
    y_s = [jnp.broadcast_to(trig[3, m : m + 1, :], (8, ATOMS)) for m in range(TOP + 1)]

    def put_wave(group, c, s):
        tile, row = group // 24, (group % 24) * 8
        wave_f[tile, row : row + 8, 0:ATOMS] = c
        wave_f[tile, row : row + 8, ATOMS : 2 * ATOMS] = s

    for kx in range(-TOP, TOP + 1):
        x_c = trig[0, abs(kx) : abs(kx) + 1, :]
        x_s = trig[1, abs(kx) : abs(kx) + 1, :]
        if kx < 0:
            x_s = -x_s
        xz_c = x_c * z_c - x_s * z_s
        xz_s = x_c * z_s + x_s * z_c
        base = (kx + TOP) * SIDE + TOP
        put_wave(base, xz_c, xz_s)
        for ky in range(1, TOP + 1):
            cc, ss = xz_c * y_c[ky], xz_s * y_s[ky]
            cs, sc = xz_c * y_s[ky], xz_s * y_c[ky]
            put_wave(base + ky, cc - ss, cs + sc)
            put_wave(base - ky, cc + ss, sc - cs)
    for group in range(SIDE * SIDE, SLOTS // 8):
        put_wave(group, jnp.zeros((8, ATOMS), F32), jnp.zeros((8, ATOMS), F32))

    half = iota((ATOMS, ATOMS), 1) < 64
    q_h, q_l = split(
        jnp.concatenate([jnp.where(half, charge, 0.0), jnp.where(half, 0.0, charge)], axis=0)
    )
    acc[0:128, :] = jnp.zeros((128, 128), F32)
    acc[128:256, :] = jnp.zeros((128, 128), F32)
    acc[0:8, :] = z_c * live_row
    acc[64:72, :] = z_s * live_row
    acc[128:136, :] = -(z_s * live_row)
    acc[192:200, :] = z_c * live_row
    live_rhs = jnp.concatenate(
        [jnp.transpose(acc[0:128, :]), jnp.transpose(acc[128:256, :])], axis=0
    )
    l_h, l_l = split(live_rhs)
    both_h = jnp.concatenate([q_h, l_h], axis=1)
    both_l = jnp.concatenate([q_l, l_l], axis=1)
    spare = lax.rem(iota((ROWS, 128), 0), 8) == 7

    @pl.loop(0, TILES)
    def _(t):
        w_h, w_l = split(wave_f[t])
        wave_h[t] = w_h
        wave_l[t] = w_l
        sums = dot3(w_h, w_l, both_h, both_l)
        part1[t] = jnp.where(spare, sums[:, 128:256], sums[:, 0:128]).astype(BF16)

    pl.semaphore_wait(barrier, 3 * (EDGE - 1))

    def totals(axis, stage, source):
        copies = []
        for d in range(1, EDGE):
            copies.append(
                send(
                    source,
                    gott.at[stage, d - 1],
                    tsend.at[stage, d - 1],
                    trecv.at[stage, d - 1],
                    device_at(axis, d)[1],
                )
            )
        return copies

    def gathered_totals(copies, stage, source):
        arrive(copies)
        value = source[...]
        for d in range(1, EDGE):
            value = value + gott[stage, d - 1]
        return value

    def shift(axis, stage, kind, buffer, source, before, after, width):
        ring = []
        for side, distance in ((0, 1), (1, EDGE - 1)):
            start = before if side == 0 else after
            ring.append(
                send(
                    buffer.at[pl.ds(source, width)] if width > 1 else buffer.at[source],
                    buffer.at[pl.ds(start, width)] if width > 1 else buffer.at[start],
                    hsend.at[kind, stage, side],
                    hrecv.at[kind, stage, side],
                    device_at(axis, distance)[1],
                )
            )
        return ring

    def halo(stage, kind, buffer):
        if stage == 0:
            return shift(2, 0, kind, buffer, 13, 12, 14, 1)
        if stage == 1:
            return shift(0, 1, kind, buffer, 12, 9, 15, 3)
        return shift(1, 2, kind, buffer, 9, 0, 18, 9)

    red_z = spread(2, 0, lambda peer: part1.at[peer], lambda s: got1z.at[s])
    tot_z = totals(2, 0, tot0)
    halo_f = halo(0, 0, nfeat)
    halo_p = halo(0, 1, npos)

    k_h, k_l = split(kf_ref[...])
    kf2 = jnp.concatenate([k_h, k_l], axis=0)
    kx, ky, kz = kidx_ref[0:1, :], kidx_ref[1:2, :], kidx_ref[2:3, :]
    sign = jnp.where(kz < 0, -1, 1)
    slot = ((kx * sign + TOP) * SIDE + (ky * sign + TOP)) * 8 + kz * sign
    scale = 4.0 / math.sqrt(ATOMS * EDGE * EDGE * EDGE * WAVES)

    @pl.loop(0, TILES)
    def _(t):
        hot = jnp.where(iota((ROWS, WAVES), 0) + t * ROWS == slot, 1.0, 0.0).astype(BF16)
        part = dot(hot, kf2, NT)
        filt[t] = (part + pltpu.roll(part, 64, axis=1)) * scale

    for axis in range(3):
        pcol[axis] = jnp.transpose(jnp.broadcast_to(pos_ref[axis : axis + 1, :], (ATOMS, ATOMS)))
    acc[0:ATOMS, :] = jnp.zeros((ATOMS, CHANNELS), F32)
    for b in range(BASES):
        wcat[:, b * CHANNELS : b * CHANNELS + CHANNELS] = wproj_ref[b]

    def pair(q, oz, row0, rows):
        where = npos[q * 3 + oz]
        shift_y = (q // 3 - 1).astype(F32)
        shift_x = (lax.rem(q, 3) - 1).astype(F32)
        dx = (where[0:1, :] + shift_x) - pcol[0, row0 : row0 + rows, :]
        dy = (where[1:2, :] + shift_y) - pcol[1, row0 : row0 + rows, :]
        dz = (where[2:3, :] + float(oz - 1)) - pcol[2, row0 : row0 + rows, :]
        scaled = (dx * dx + dy * dy + dz * dz) * (1.0 / CUTOFF2)
        base = jnp.maximum(1.0 - scaled, 0.0)
        if oz == 1:
            same = iota((rows, ATOMS), 0) + row0 == iota((rows, ATOMS), 1)
            base = base * jnp.where(same, jnp.where(q == 4, 0.0, 1.0), 1.0)
        e1 = jnp.exp(-scaled)
        e2 = e1 * e1
        e3 = e2 * e1
        e4 = e2 * e2
        e8 = e4 * e4
        e20 = e8 * e8 * e4
        return dx, dy, dz, base, (e1, e3, e8, e20)

    STRIP = 32

    def message_block(q):
        for oz in range(3):
            for row0 in range(0, ATOMS, STRIP):
                _, _, _, base, decay = pair(q, oz, row0, STRIP)
                envelope = base * base
                for b in range(BASES):
                    column = (oz * BASES + b) * ATOMS
                    rad[row0 : row0 + STRIP, column : column + ATOMS] = (
                        decay[b] * envelope
                    ).astype(BF16)
            values = dot(nfeat[q * 3 + oz], wcat[...]).astype(BF16)
            for b in range(BASES):
                nbasis[q * 3 + oz, b * ATOMS : b * ATOMS + ATOMS, :] = values[
                    :, b * CHANNELS : b * CHANNELS + CHANNELS
                ]
        near = nbasis[pl.ds(q * 3, 3)].reshape(3 * BASES * ATOMS, CHANNELS)
        acc[0:ATOMS, :] += dot(rad[...], near)

    def reduced(own_part, got):
        value = own_part.astype(F32)
        for d in range(1, EDGE):
            value = value + got[d - 1].astype(F32)
        return value

    arrive(red_z)
    value = reduced(part1[me[2]], got1z)
    for c in range(EDGE):
        mid1[c] = value[c * CHUNK : c * CHUNK + CHUNK, :]
    red_y = spread(1, 1, lambda peer: mid1.at[peer], lambda s: got1y.at[s])
    tot1[...] = gathered_totals(tot_z, 0, tot0)
    tot_y = totals(1, 1, tot1)
    arrive(halo_f)
    arrive(halo_p)
    halo_f = halo(1, 0, nfeat)
    halo_p = halo(1, 1, npos)
    message_block(jnp.int32(4))

    arrive(red_y)
    low1[...] = reduced(mid1[me[1]], got1y)
    red_x = spread(0, 2, lambda peer: low1, lambda s: got1x.at[s])
    tot2[...] = gathered_totals(tot_y, 1, tot1)
    tot_x = totals(0, 2, tot2)
    arrive(halo_f)
    arrive(halo_p)
    halo_f = halo(2, 0, nfeat)
    halo_p = halo(2, 1, npos)
    message_block(jnp.int32(3))
    message_block(jnp.int32(5))

    arrive(red_x)
    value = reduced(low1[...], got1x)
    total = gathered_totals(tot_x, 2, tot2)
    mean = total[0:1, :] / total[1:2, :]
    lane8 = iota((8, 128), 1)
    row8 = iota((8, 128), 0)
    for g in range(CHUNK // 8):
        tile = value[g * 8 : g * 8 + 8, :]
        live = jnp.broadcast_to(tile[7:8, :], (8, 128))
        live_c = jnp.sum(jnp.where(lane8 == row8, live, 0.0), axis=1, keepdims=True)
        live_s = jnp.sum(jnp.where(lane8 == row8 + 64, live, 0.0), axis=1, keepdims=True)
        up1[me[1], g * 8 : g * 8 + 8, :] = tile - jnp.where(lane8 < 64, live_c, live_s) * mean
    out_y = spread(1, 3, lambda peer: up1.at[me[1]], lambda s: up1.at[me[1]])
    arrive(halo_f)
    arrive(halo_p)

    @pl.loop(0, 3)
    def _(q):
        message_block(q)

    arrive(out_y)
    all1[me[2]] = jnp.concatenate([up1[c] for c in range(EDGE)], axis=0).astype(BF16)
    out_z = spread(2, 4, lambda peer: all1.at[me[2]], lambda s: all1.at[me[2]])

    @pl.loop(6, 9)
    def _(q):
        message_block(q)

    pre_near = dot(acc[0:ATOMS, :].astype(BF16), wmix_ref[...])
    uv[:, CHANNELS : 2 * CHANNELS] = nbasis[13]

    arrive(out_z)
    prod[0:128, 0:256] = jnp.zeros((128, 256), F32)

    @pl.loop(0, TILES)
    def _(t):
        f_h, f_l = split(filt[t] * all1[t].astype(F32))
        fs_h[t] = f_h
        fs_l[t] = f_l
        prod[0:128, 0:256] += dot3(f_h, f_l, wave_h[t], wave_l[t], TN)

    potential = prod[0:64, 0:128] + prod[64:128, 128:256]
    pre = pre_near + dot(potential.astype(BF16), wlong_ref[...], TN)
    gate = sigmoid(pre)
    refined = own.astype(F32) + pre * gate
    upd_ref[...] = refined.astype(BF16)
    outer = sigmoid(refined)
    readout = rows_ref[1:2, :]
    energy_col = jnp.sum(refined * outer * readout, axis=1, keepdims=True)
    energy_ref[...] = (
        jnp.transpose(jnp.broadcast_to(energy_col, (ATOMS, ATOMS)))[0:1, :] * live_row
    )
    grad_new = live_col * readout * (outer * (1.0 + refined * (1.0 - outer)))
    grad_pre = (grad_new * (gate * (1.0 + pre * (1.0 - gate)))).astype(BF16)
    adjoint = dot(grad_pre, wmix_ref[...], NT).astype(BF16)
    nadj[13] = adjoint
    halo_a = halo(0, 2, nadj)
    wlong2 = jnp.concatenate([wlong_ref[...], wlong_ref[...]], axis=0)
    pull_rows = dot(grad_pre, wlong2, NT)
    p_h, p_l = split(
        jnp.concatenate(
            [jnp.where(half, pull_rows, 0.0), jnp.where(half, 0.0, pull_rows)], axis=0
        )
    )

    @pl.loop(0, TILES)
    def _(t):
        part2[t] = dot3(wave_h[t], wave_l[t], p_h, p_l).astype(BF16)

    red_z = spread(2, 5, lambda peer: part2.at[peer], lambda s: got2z.at[s])

    first = iota((ATOMS, ATOMS), 0) < 64
    pull_t = jnp.transpose(pull_rows)
    neutral_t = jnp.transpose((charge - mean) * live_col)
    pull[0:128, 0:128] = jnp.where(first, 0.0, pull_t)
    pull[0:128, 128:256] = jnp.where(first, pull_t, 0.0)
    pull[128:256, 0:128] = jnp.where(first, 0.0, neutral_t)
    pull[128:256, 128:256] = jnp.where(first, neutral_t, 0.0)

    for b in range(BASES):
        uv[b * ATOMS : b * ATOMS + ATOMS, 0:CHANNELS] = adjoint
    for axis in range(3):
        acc[axis * ATOMS : axis * ATOMS + ATOMS, :] = jnp.zeros((ATOMS, ATOMS), F32)

    def force_block(q):
        for oz in range(3):
            for b in range(BASES):
                rows = slice(b * ATOMS, b * ATOMS + ATOMS)
                near = jnp.concatenate([nbasis[q * 3 + oz, rows, :], nadj[q * 3 + oz]], axis=1)
                prod[rows, oz * 128 : oz * 128 + 128] = dot(uv[rows, :], near, NT)
        for row0 in range(0, ATOMS, STRIP):
            total_x = total_y = total_z = None
            for oz in range(3):
                dx, dy, dz, base, decay = pair(q, oz, row0, STRIP)
                envelope = base * base
                double = base + base
                strength = None
                for b, rate in enumerate((1.0, 3.0, 8.0, 20.0)):
                    got = prod[
                        b * ATOMS + row0 : b * ATOMS + row0 + STRIP, oz * 128 : oz * 128 + 128
                    ]
                    term = decay[b] * (envelope * rate + double) * got
                    strength = term if strength is None else strength + term
                if total_x is None:
                    total_x, total_y, total_z = strength * dx, strength * dy, strength * dz
                else:
                    total_x = total_x + strength * dx
                    total_y = total_y + strength * dy
                    total_z = total_z + strength * dz
            acc[row0 : row0 + STRIP, :] += total_x
            acc[128 + row0 : 128 + row0 + STRIP, :] += total_y
            acc[256 + row0 : 256 + row0 + STRIP, :] += total_z

    arrive(halo_a)
    halo_a = halo(1, 2, nadj)
    force_block(jnp.int32(4))

    arrive(red_z)
    value = reduced(part2[me[2]], got2z)
    for c in range(EDGE):
        mid2[c] = value[c * CHUNK : c * CHUNK + CHUNK, :]
    red_y = spread(1, 6, lambda peer: mid2.at[peer], lambda s: got2y.at[s])
    arrive(halo_a)
    halo_a = halo(2, 2, nadj)
    force_block(jnp.int32(3))
    force_block(jnp.int32(5))

    arrive(red_y)
    low2[...] = reduced(mid2[me[1]], got2y)
    red_x = spread(0, 7, lambda peer: low2, lambda s: got2x.at[s])
    arrive(halo_a)

    @pl.loop(0, 2)
    def _(q):
        force_block(q)

    arrive(red_x)
    up2[me[1]] = reduced(low2[...], got2x)
    out_y = spread(1, 8, lambda peer: up2.at[me[1]], lambda s: up2.at[me[1]])

    @pl.loop(0, 2)
    def _(q):
        force_block(q * 4 + 2)

    arrive(out_y)
    all2[me[2]] = jnp.concatenate([up2[c] for c in range(EDGE)], axis=0).astype(BF16)
    out_z = spread(2, 9, lambda peer: all2.at[me[2]], lambda s: all2.at[me[2]])

    @pl.loop(7, 9)
    def _(q):
        force_block(q)

    lane = iota((ATOMS, ATOMS), 1)
    columns = jnp.zeros((ATOMS, ATOMS), F32)
    for axis in range(3):
        near_sum = jnp.sum(acc[axis * ATOMS : axis * ATOMS + ATOMS, :], axis=1, keepdims=True)
        columns = jnp.where(lane == axis, near_sum, columns)
    near_force = jnp.transpose(columns)[0:8, :] * (-2.0 / CUTOFF2)
    r_h, r_l = split(pull[...])

    arrive(out_z)
    prod[0:8, 0:128] = jnp.zeros((8, 128), F32)

    @pl.loop(0, TILES)
    def _(t):
        b_h, b_l = split(filt[t] * all2[t].astype(F32))
        left_h = jnp.concatenate([fs_h[t], b_h], axis=1)
        left_l = jnp.concatenate([fs_l[t], b_l], axis=1)
        mixed = dot3(left_h, left_l, r_h, r_l)
        waves = wave_f[t]
        d_h, d_l = split(
            waves[:, 0:128] * mixed[:, 0:128] - waves[:, 128:256] * mixed[:, 128:256]
        )
        index = iota((8, ROWS), 1) + t * ROWS
        axis_row = iota((8, ROWS), 0)
        group = lax.shift_right_logical(index, 3)
        group_x = lax.shift_right_logical(group * 79, 10)
        value_x = group_x - TOP
        value_y = group - group_x * SIDE - TOP
        value_z = lax.bitwise_and(index, 7)
        values = jnp.where(axis_row == 0, value_x, jnp.where(axis_row == 1, value_y, value_z))
        rows = values.astype(F32).astype(BF16)
        prod[0:8, 0:128] += dot(rows, d_h) + dot(rows, d_l)

    force = near_force - prod[0:8, 0:128] * (2.0 * math.pi / EDGE)
    force_ref[...] = force[0:3, :]
    for copy in sent:
        copy.wait_send()


def shards(
    features,
    positions,
    counts,
    w_proj,
    w_mix,
    w_long,
    w_charge,
    charge_bias,
    w_energy,
    k_filter,
    k_index,
):
    rows = jnp.stack([jnp.concatenate([charge_bias, charge_bias]), w_energy])
    vmem = pl.BlockSpec(memory_space=pltpu.VMEM)
    dma = pltpu.SemaphoreType.DMA
    reduce_buffers = [
        pltpu.VMEM((TILES, ROWS, 128), BF16),
        pltpu.VMEM((EDGE - 1, ROWS, 128), BF16),
        pltpu.VMEM((EDGE, CHUNK, 128), F32),
        pltpu.VMEM((EDGE - 1, CHUNK, 128), F32),
        pltpu.VMEM((CHUNK, 128), F32),
        pltpu.VMEM((EDGE - 1, CHUNK, 128), F32),
        pltpu.VMEM((EDGE, CHUNK, 128), F32),
        pltpu.VMEM((TILES, ROWS, 128), BF16),
    ]
    updated, energy, force = pl.pallas_call(
        block_kernel,
        name="block",
        out_shape=(
            jax.ShapeDtypeStruct((ATOMS, CHANNELS), BF16),
            jax.ShapeDtypeStruct((1, ATOMS), F32),
            jax.ShapeDtypeStruct((3, ATOMS), F32),
        ),
        in_specs=[pl.BlockSpec(memory_space=pltpu.SMEM)] + [vmem] * 9,
        out_specs=(vmem, vmem, vmem),
        scratch_shapes=[
            pltpu.VMEM((27, ATOMS, CHANNELS), BF16),
            pltpu.VMEM((27, ATOMS, CHANNELS), BF16),
            pltpu.VMEM((27, 8, ATOMS), F32),
            pltpu.VMEM((6, 8, ATOMS), F32),
            pltpu.VMEM((TILES, ROWS, 256), F32),
            pltpu.VMEM((TILES, ROWS, 256), BF16),
            pltpu.VMEM((TILES, ROWS, 256), BF16),
            pltpu.VMEM((TILES, ROWS, 128), F32),
            pltpu.VMEM((TILES, ROWS, 128), BF16),
            pltpu.VMEM((TILES, ROWS, 128), BF16),
        ]
        + reduce_buffers
        + reduce_buffers
        + [
            pltpu.VMEM((8, 128), F32),
            pltpu.VMEM((8, 128), F32),
            pltpu.VMEM((8, 128), F32),
            pltpu.VMEM((3, EDGE - 1, 8, 128), F32),
            pltpu.VMEM((3, ATOMS, ATOMS), F32),
            pltpu.VMEM((ATOMS, 3 * BASES * ATOMS), BF16),
            pltpu.VMEM((CHANNELS, BASES * CHANNELS), BF16),
            pltpu.VMEM((27, BASES * ATOMS, CHANNELS), BF16),
            pltpu.VMEM((BASES * ATOMS, CHANNELS), F32),
            pltpu.VMEM((BASES * ATOMS, 3 * 128), F32),
            pltpu.VMEM((BASES * ATOMS, 2 * CHANNELS), BF16),
            pltpu.VMEM((256, 256), F32),
            dma((10, EDGE - 1)),
            dma((10, EDGE - 1)),
            dma((3, EDGE - 1)),
            dma((3, EDGE - 1)),
            dma((3, 3, 2)),
            dma((3, 3, 2)),
        ],
        compiler_params=pltpu.CompilerParams(
            collective_id=0, has_side_effects=True, vmem_limit_bytes=48 * 1024 * 1024
        ),
    )(
        counts.reshape(1),
        features[0, 0, 0],
        positions[0, 0, 0],
        w_proj,
        w_mix,
        w_long,
        w_charge,
        rows,
        k_filter,
        k_index,
    )
    return (
        updated[None, None, None],
        energy.reshape(1, 1, 1, ATOMS),
        force[None, None, None],
    )


def solution(mesh):
    cells = P("gx", "gy", "gz")
    in_specs = (cells, cells, cells) + (P(),) * 8
    return jax.shard_map(
        shards, mesh=mesh, in_specs=in_specs, out_specs=(cells, cells, cells), check_vma=False
    )
```

time: 675 us -> 99 us (0.15); the launches traced: 663 us -> 98.4 us
  waiting for transfers between devices: 337 us -> 0 us
  blocking collectives: 101 us -> 0 us
  Pallas kernels: 0 us -> 88.3 us
  matrix products: 87.7 us -> 0 us
  starting transfers between devices: 60.2 us -> 0 us
  other arithmetic: 34.2 us -> 1.47 us
  between operations: 16.3 us -> 1.32 us
  local copies, waits for them, and re-layouts: 18.9 us -> 7.31 us
  loops' own time: 7.66 us -> 0 us
    psum x2 -> x0, waiting for transfers between devices: 314 us -> none  [the longest x1 195 us: shards(): back_c, back_s = lax.psum((pull_c, pull_s), ('gx', 'gy', 'gz'))]
    psum x1 -> x0, blocking collectives: 101 us -> none  [shards(): lax.psum((local_c, local_s, jnp.sum(charges, axis=1), jnp.sum(living)), (...]
    pallas_call x0 -> x1, Pallas kernels: none -> 88.3 us  [shards(): pl.pallas_call(block_kernel, name='block', out_shape=(jax.ShapeDtypeStruc...]
    dot_general x150 -> x0, matrix products: 87.7 us -> none  [the longest x27 26 us: add_force(): jnp.einsum('bic,jc->ibj', local_proj, near_rows, preferred_element_type=j...]
    ppermute x18 -> x0, starting transfers between devices: 60.1 us -> none  [the longest x9 33 us: extended(): after = lax.ppermute(initial, axis, down)]
    ppermute x18 -> x0, waiting for transfers between devices: 22.5 us -> none  [the longest x9 19.4 us: extended(): before = lax.ppermute(last, axis, up)]
    reduce_sum x82 -> x0, other arithmetic: 13.2 us -> none  [the longest x54 6.37 us: pair_geometry(): scaled = jnp.sum(offset_vec * offset_vec, axis=0) / (CUTOFF * CUTOFF)]
    another operation x2 -> x0, loops' own time: 7.66 us -> none  [the longest x1 4.75 us: shards(): lax.fori_loop(0, 27, add_force, jnp.zeros((3, atom_count), jnp.float32))]
  transfers between devices with their start and end apart: 20 -> 0, of which waited for: 7 -> 0; matrix products, arithmetic and copies ran while one was open for 16% -> 0% of each run, Pallas kernels for 0% -> 0%
where the time goes in v1:
time: 99 us; the launch traced here: 98.4 us
  Pallas kernels  88.3 us (89%)
  local copies, waits for them, and re-layouts  7.31 us (7%)
  other arithmetic  1.47 us (1%)
  between operations  1.32 us (1%)
    pallas_call x1, Pallas kernels, shards(): pl.pallas_call(block_kernel, name='block', out_shape=(jax.ShapeDtypeStruc...  88.3 us
    unnamed x18, local copies, waits for them, and re-layouts  7.31 us

profile of v1, /device:TPU:1, one launch (start us, length us, event | category | flops | bytes accessed | tf_op | source)
XLA Modules:
  0.0 98.4 jit_solution(18092977947970314063)
XLA Ops:
  0.6 0.0 copy-start.5
  1.3 0.8 maximum_bitcast_fusion
  2.1 0.7 pad_maximum_fusion.rows_ref
  2.8 0.7 copy.17
  3.5 0.0 copy-done.5
  3.5 0.0 copy-start
  3.5 1.0 %copy-done = f32[64,2048]{1,0:T(8,128)S(1)} copy-done((f32[64,2048]{1,0:T(8,128)S(1)}, f32[64,2048]{1,0:T(8,128)}, u32[]{:S(2)}) %copy-start) | copy-done | bytes 524312
  4.5 0.0 copy-start.1
  4.5 0.9 copy-done.1
  5.4 0.0 copy-start.2
  5.4 0.8 copy-done.2
  6.2 0.0 copy-start.3
  6.2 0.8 copy-done.3
  6.9 0.0 copy-start.4
  6.9 0.8 copy-done.4
  7.7 0.0 copy-start.6
  7.7 0.7 copy-done.6
  8.4 88.3 %block.1 = (bf16[128,128]{1,0:T(8,128)(2,1)S(1)}, f32[1,128]{1,0:T(1,128)S(1)}, f32[3,128]{1,0:T(4,128)S(1)}) custom-call(s32[1]{0:T(128)} %bitcast.11.counts_ref, bf16[128,128]{1,0:T(8,128)(2,1)S(1)} %bitcast.12, f32[3,128]{1,0:T(4,128)S(1)} %bitcast.14, bf16[4,128,128]{2,1,0:T(8,128)(2,1)S(1)} %copy-done.1, bf16[128,128]{1,0:T(8,128)(2,1)S(1)} %copy-done.3, ...), custom_call_target="tpu_custom_call" | custom-call | tf_op jit(solution)/shard_map/block/pallas_call | solution.py:591
  96.7 0.6 copy.14
  97.3 0.6 copy.21
  97.9 0.5 copy.22
Async XLA Ops:
  0.6 2.8 %copy-start.5 = (bf16[64,128]{1,0:T(8,128)(2,1)S(1)}, bf16[64,128]{1,0:T(8,128)(2,1)}, u32[]{:S(2)}) copy-start(bf16[64,128]{1,0:T(8,128)(2,1)} %wlong_ref.1) | copy-start | bytes 49156
  3.5 1.0 %copy-start = (f32[64,2048]{1,0:T(8,128)S(1)}, f32[64,2048]{1,0:T(8,128)}, u32[]{:S(2)}) copy-start(f32[64,2048]{1,0:T(8,128)} %kf_ref.1) | copy-start | bytes 1572868
  4.5 0.9 copy-start.1
  5.4 0.8 copy-start.2
  6.2 0.8 copy-start.3
  6.9 0.8 copy-start.4
  7.7 0.7 copy-start.6

commit v2 on v1

v2 whole, which is shorter than its diff:
```python
import functools
import math

import jax
import jax.numpy as jnp
from jax import lax
from jax.experimental import pallas as pl
from jax.experimental.pallas import tpu as pltpu
from jax.sharding import PartitionSpec as P

MESH = pl.DeviceIdType.MESH
CUTOFF2 = 0.9 * 0.9
ATOMS = 128
CHANNELS = 128
BASES = 4
EDGE = 8
WAVES = 2048
TOP = 6
SIDE = 2 * TOP + 1
TILES = 8
ROWS = 192
PIECES = 1
PIECE = 192
SUB = 24
SLOTS = TILES * ROWS
F32 = jnp.float32
BF16 = jnp.bfloat16
NT = (((1,), (1,)), ((), ()))
NN = (((1,), (0,)), ((), ()))
TN = (((0,), (0,)), ((), ()))


def dot(a, b, dims=NN):
    return lax.dot_general(a, b, dims, preferred_element_type=F32)


def split(value):
    high = value.astype(BF16)
    low = (value - high.astype(F32)).astype(BF16)
    return high, low


def dot3(a_high, a_low, b_high, b_low, dims=NN):
    return dot(a_high, b_high, dims) + dot(a_high, b_low, dims) + dot(a_low, b_high, dims)


def iota(shape, dim):
    return lax.broadcasted_iota(jnp.int32, shape, dim)


def sigmoid(v):
    return 1.0 / (1.0 + jnp.exp(-v))


def block_kernel(
    counts_ref,
    feat_hbm,
    pos_hbm,
    wproj_hbm,
    wmix_hbm,
    wlong_hbm,
    wcharge_hbm,
    bias_hbm,
    wenergy_hbm,
    kf_hbm,
    kidx_hbm,
    upd_ref,
    energy_ref,
    force_ref,
    feat_ref,
    pos_ref,
    wproj_ref,
    wmix_ref,
    wlong_ref,
    wcharge_ref,
    bias_ref,
    wenergy_ref,
    kf_ref,
    kidx_ref,
    nfeat,
    nadj,
    pack,
    trig,
    row,
    wave_f,
    wave_h,
    wave_l,
    filt,
    fs_h,
    fs_l,
    part1,
    gotz1,
    mid1,
    goty1,
    low1,
    gotx1,
    up1,
    full1,
    part2,
    gotz2,
    mid2,
    goty2,
    low2,
    gotx2,
    up2,
    full2,
    pcol,
    rad,
    wcat,
    nbasis,
    acc,
    prod,
    uv,
    pull,
    load_sem,
    send_sem,
    recv_sem,
    hsend,
    hrecv,
):
    me = tuple(lax.axis_index(name) for name in ("gx", "gy", "gz"))

    zcore, yrow, xhalf = lax.rem(me[0], 2), me[1], lax.rem(me[2], 2)
    place = ((me[0] // 2) * 2 + xhalf, yrow, (me[2] // 2) * 2 + zcore)

    def device_at(axis, distance):
        peer = lax.rem(place[axis] + distance, EDGE)
        high, low = (peer // 2) * 2, lax.rem(peer, 2)
        if axis == 0:
            return peer, (high + zcore, me[1], (me[2] // 2) * 2 + low)
        if axis == 1:
            return peer, (me[0], peer, me[2])
        return peer, ((me[0] // 2) * 2 + low, me[1], high + xhalf)

    def cell_at(axis, distance):
        coords = list(me)
        coords[axis] = lax.rem(me[axis] + distance, EDGE)
        return tuple(coords)

    loads = [
        pltpu.make_async_copy(source, target, load_sem.at[i])
        for i, (source, target) in enumerate(
            (
                (pos_hbm, pos_ref),
                (feat_hbm, feat_ref),
                (wcharge_hbm, wcharge_ref),
                (bias_hbm, bias_ref),
                (kidx_hbm, kidx_ref),
                (kf_hbm, kf_ref),
                (wproj_hbm, wproj_ref),
                (wmix_hbm, wmix_ref),
                (wlong_hbm, wlong_ref),
                (wenergy_hbm, wenergy_ref),
            )
        )
    ]
    for load in loads:
        load.start()
    barrier = pltpu.get_barrier_semaphore()
    for axis in range(3):
        for d in range(1, EDGE):
            pl.semaphore_signal(
                barrier, inc=1, device_id=device_at(axis, d)[1], device_id_type=MESH
            )

    for axis in (0, 2):
        for d in (1, EDGE - 1):
            pl.semaphore_signal(
                barrier, inc=1, device_id=cell_at(axis, d), device_id_type=MESH
            )

    sent = []

    def drain():
        for copy in sent:
            copy.wait_send()
        sent.clear()

    def send(src, dst, ssem, rsem, device):
        copy = pltpu.make_async_remote_copy(
            src_ref=src,
            dst_ref=dst,
            send_sem=ssem,
            recv_sem=rsem,
            device_id=device,
            device_id_type=MESH,
        )
        copy.start()
        sent.append(copy)
        return copy

    def spread(axis, slot, source, target):
        copies = []
        for d in range(1, EDGE):
            peer, device = device_at(axis, d)
            copies.append(
                send(
                    source(peer),
                    target(d - 1),
                    send_sem.at[slot + (d - 1,)],
                    recv_sem.at[slot + (d - 1,)],
                    device,
                )
            )
        return copies

    def arrive(copies):
        for copy in copies:
            copy.wait_recv()

    def tile_at(distance):
        return lax.rem(place[2] + distance, EDGE)

    def send_tile(kind, part, gotz, d):
        peer, device = device_at(2, d)
        copies = []
        for p in range(PIECES):
            rows = pl.ds(p * PIECE, PIECE)
            copies.append(
                send(
                    part.at[peer, rows],
                    gotz.at[d - 1, rows],
                    send_sem.at[kind, 0, p, d - 1],
                    recv_sem.at[kind, 0, p, d - 1],
                    device,
                )
            )
        return copies

    def reduce_gather(kind, tiles, part, gotz, mid, goty, low, gotx, up, full, finish, hook):
        stages = []
        for p in range(PIECES):
            arrive([copies[p] for copies in tiles])
            rows = slice(p * PIECE, p * PIECE + PIECE)
            value = part[place[2], rows, :].astype(F32)
            for d in range(1, EDGE):
                value = value + gotz[d - 1, rows, :].astype(F32)
            for c in range(EDGE):
                mid[p, c] = value[c * SUB : c * SUB + SUB, :]
            stages.append(
                spread(
                    1, (kind, 1, p), lambda peer: mid.at[p, peer], lambda s: goty.at[s, p]
                )
            )
        hook(0)
        copies, stages = stages, []
        for p in range(PIECES):
            arrive(copies[p])
            value = mid[p, place[1]]
            for d in range(1, EDGE):
                value = value + goty[d - 1, p]
            low[p] = value
            stages.append(
                spread(0, (kind, 2, p), lambda peer: low.at[p], lambda s: gotx.at[s, p])
            )
        hook(1)
        copies, stages = stages, []
        for p in range(PIECES):
            arrive(copies[p])
            value = low[p]
            for d in range(1, EDGE):
                value = value + gotx[d - 1, p]
            up[p, place[1]] = finish(value).astype(BF16)
            stages.append(
                spread(
                    1, (kind, 3, p), lambda peer: up.at[p, place[1]], lambda s: up.at[p, place[1]]
                )
            )
        hook(2)
        copies, stages = stages, []
        for p in range(PIECES):
            arrive(copies[p])
            rows = pl.ds(p * PIECE, PIECE)
            full[place[2], p * PIECE : p * PIECE + PIECE, :] = jnp.concatenate(
                [up[p, c].astype(F32) for c in range(EDGE)], axis=0
            ).astype(BF16)
            stages.append(
                spread(
                    2,
                    (kind, 4, p),
                    lambda peer: full.at[place[2], rows],
                    lambda s: full.at[place[2], rows],
                )
            )
        hook(3)
        return stages

    live_row = (iota((1, ATOMS), 1) < counts_ref[0]).astype(F32)
    live_col = (iota((ATOMS, CHANNELS), 0) < counts_ref[0]).astype(F32)
    row[...] = jnp.zeros((8, 128), F32)
    pack[...] = jnp.zeros((16, 128), F32)
    loads[0].wait()

    steps = iota((8, ATOMS), 0).astype(F32)
    for axis in range(3):
        unit = (pos_ref[axis] + me[axis].astype(F32)) * (1.0 / EDGE)
        orders = steps if axis < 2 else jnp.where(steps > 6.5, 0.0, steps)
        turns = orders * unit
        angle = (turns - jnp.floor(turns + 0.5)) * (2.0 * math.pi)
        trig[2 * axis] = jnp.cos(angle)
        trig[2 * axis + 1] = jnp.sin(angle)
    loads[1].wait()
    loads[2].wait()
    loads[3].wait()
    own = feat_ref[...]
    masked = own * live_col.astype(BF16)
    nfeat[13, 0:ATOMS, :] = masked
    for axis in range(3):
        rest = pos_ref[axis]
        for step in range(3):
            digit = rest.astype(BF16).astype(F32)
            pack[3 * step + axis : 3 * step + axis + 1, :] = digit
            rest = rest - digit
    nfeat[13, ATOMS : ATOMS + 16, :] = pack[...].astype(BF16)

    wcharge2 = jnp.concatenate([wcharge_ref[...], wcharge_ref[...]], axis=0)
    row[0:1, 0:64] = bias_ref[...]
    bias = row[...]
    charge_pre = dot(masked, wcharge2, NT) + (bias + pltpu.roll(bias, 64, axis=1))[0:1, :]
    charge = charge_pre * sigmoid(charge_pre) * live_col
    own_total = jnp.broadcast_to(jnp.sum(charge, axis=0, keepdims=True), (8, 128))
    own_count = jnp.broadcast_to(jnp.sum(live_col, axis=0, keepdims=True), (8, 128))
    z_c = trig[4]
    z_s = trig[5]
    y_c = [jnp.broadcast_to(trig[2, m : m + 1, :], (8, ATOMS)) for m in range(TOP + 1)]
    y_s = [jnp.broadcast_to(trig[3, m : m + 1, :], (8, ATOMS)) for m in range(TOP + 1)]

    def put_wave(group, c, s):
        tile, row = group // 24, (group % 24) * 8
        wave_f[tile, row : row + 8, 0:ATOMS] = c
        wave_f[tile, row : row + 8, ATOMS : 2 * ATOMS] = s

    for kx in range(-TOP, TOP + 1):
        x_c = trig[0, abs(kx) : abs(kx) + 1, :]
        x_s = trig[1, abs(kx) : abs(kx) + 1, :]
        if kx < 0:
            x_s = -x_s
        xz_c = x_c * z_c - x_s * z_s
        xz_s = x_c * z_s + x_s * z_c
        base = (kx + TOP) * SIDE + TOP
        put_wave(base, xz_c, xz_s)
        for ky in range(1, TOP + 1):
            cc, ss = xz_c * y_c[ky], xz_s * y_s[ky]
            cs, sc = xz_c * y_s[ky], xz_s * y_c[ky]
            put_wave(base + ky, cc - ss, cs + sc)
            put_wave(base - ky, cc + ss, sc - cs)
    for group in range(SIDE * SIDE, SLOTS // 8):
        put_wave(group, jnp.zeros((8, ATOMS), F32), jnp.zeros((8, ATOMS), F32))

    half = iota((ATOMS, ATOMS), 1) < 64
    q_h, q_l = split(
        jnp.concatenate([jnp.where(half, charge, 0.0), jnp.where(half, 0.0, charge)], axis=0)
    )
    acc[0:128, :] = jnp.zeros((128, 128), F32)
    acc[128:256, :] = jnp.zeros((128, 128), F32)
    acc[0:8, :] = z_c * live_row
    acc[64:72, :] = z_s * live_row
    acc[128:136, :] = -(z_s * live_row)
    acc[192:200, :] = z_c * live_row
    live_rhs = jnp.concatenate(
        [jnp.transpose(acc[0:128, :]), jnp.transpose(acc[128:256, :])], axis=0
    )
    l_h, l_l = split(live_rhs)
    both_h = jnp.concatenate([q_h, l_h], axis=1)
    both_l = jnp.concatenate([q_l, l_l], axis=1)
    spare = lax.rem(iota((ROWS, 128), 0), 8) == 7

    pl.semaphore_wait(barrier, 3 * (EDGE - 1) + 4)

    def shift(axis, stage, kind, buffer, source, before, after, width):
        ring = []
        for side, distance in ((0, 1), (1, EDGE - 1)):
            start = before if side == 0 else after
            tag = (kind, stage, side)
            ring.append(
                send(
                    buffer.at[pl.ds(source, width)] if width > 1 else buffer.at[source],
                    buffer.at[pl.ds(start, width)] if width > 1 else buffer.at[start],
                    hsend.at[tag],
                    hrecv.at[tag],
                    cell_at(axis, distance),
                )
            )
        return ring

    def halo(stage, kind, buffer):
        if stage == 0:
            return shift(2, 0, kind, buffer, 13, 12, 14, 1)
        if stage == 1:
            return shift(0, 1, kind, buffer, 12, 9, 15, 3)
        column = (1, 0, 2)[stage - 2] * 3
        return shift(1, stage, kind, buffer, 9 + column, column, 18 + column, 3)

    halo_f = halo(0, 0, nfeat)
    lane8 = iota((8, 128), 1)
    row8 = iota((8, 128), 0)
    moved = jnp.where(lane8 == 16, own_count, pltpu.roll(own_total, 8, axis=1))
    lanes = iota((ROWS, 128), 1)
    member = lax.rem(iota((ROWS, 128), 0), 24) // 8
    first_free = (member == 0) & (lanes >= 8) & (lanes < 64)
    second_free = (member == 1) & (lanes >= 8) & (lanes <= 16)
    extra = jnp.where(first_free, own_total[0:1, :], jnp.where(second_free, moved[0:1, :], 0.0))
    tiles = []
    for d in (4, 3, 5, 2, 6, 1, 7, 0):
        t = tile_at(d)
        w_h, w_l = split(wave_f[t])
        wave_h[t] = w_h
        wave_l[t] = w_l
        sums = dot3(w_h, w_l, both_h, both_l)
        part1[t] = jnp.where(spare, sums[:, 128:256] + extra, sums[:, 0:128]).astype(BF16)
        if d > 0:
            tiles.append(send_tile(0, part1, gotz1, d))

    for load in loads[4:]:
        load.wait()
    k_h, k_l = split(kf_ref[...])
    kf2 = jnp.concatenate([k_h, k_l], axis=0)
    kx, ky, kz = kidx_ref[0:1, :], kidx_ref[1:2, :], kidx_ref[2:3, :]
    sign = jnp.where(kz < 0, -1, 1)
    slot = ((kx * sign + TOP) * SIDE + (ky * sign + TOP)) * 8 + kz * sign
    scale = 4.0 / math.sqrt(ATOMS * EDGE * EDGE * EDGE * WAVES)

    @pl.loop(0, TILES)
    def _(t):
        hot = jnp.where(iota((ROWS, WAVES), 0) + t * ROWS == slot, 1.0, 0.0).astype(BF16)
        part = dot(hot, kf2, NT)
        filt[t] = (part + pltpu.roll(part, 64, axis=1)) * scale

    for axis in range(3):
        pcol[axis] = jnp.transpose(jnp.broadcast_to(pos_ref[axis], (ATOMS, ATOMS)))
    acc[0:ATOMS, :] = jnp.zeros((ATOMS, CHANNELS), F32)
    for b in range(BASES):
        wcat[:, b * CHANNELS : b * CHANNELS + CHANNELS] = wproj_ref[b]

    def pair(q, oz, row0, rows):
        digits = nfeat[q * 3 + oz, ATOMS : ATOMS + 16, :].astype(F32)
        where = digits[0:3, :] + (digits[3:6, :] + digits[6:9, :])
        shift_y = (q // 3 - 1).astype(F32)
        shift_x = (lax.rem(q, 3) - 1).astype(F32)
        dx = (where[0:1, :] + shift_x) - pcol[0, row0 : row0 + rows, :]
        dy = (where[1:2, :] + shift_y) - pcol[1, row0 : row0 + rows, :]
        dz = (where[2:3, :] + float(oz - 1)) - pcol[2, row0 : row0 + rows, :]
        scaled = (dx * dx + dy * dy + dz * dz) * (1.0 / CUTOFF2)
        base = jnp.maximum(1.0 - scaled, 0.0)
        if oz == 1:
            same = iota((rows, ATOMS), 0) + row0 == iota((rows, ATOMS), 1)
            base = base * jnp.where(same, jnp.where(q == 4, 0.0, 1.0), 1.0)
        e1 = jnp.exp(-scaled)
        e2 = e1 * e1
        e3 = e2 * e1
        e4 = e2 * e2
        e8 = e4 * e4
        e20 = e8 * e8 * e4
        return dx, dy, dz, base, (e1, e3, e8, e20)

    STRIP = 32

    def message_block(q):
        for oz in range(3):
            for row0 in range(0, ATOMS, STRIP):
                _, _, _, base, decay = pair(q, oz, row0, STRIP)
                envelope = base * base
                for b in range(BASES):
                    column = (oz * BASES + b) * ATOMS
                    rad[row0 : row0 + STRIP, column : column + ATOMS] = (
                        decay[b] * envelope
                    ).astype(BF16)
            values = dot(nfeat[q * 3 + oz, 0:ATOMS, :], wcat[...]).astype(BF16)
            for b in range(BASES):
                nbasis[q * 3 + oz, b * ATOMS : b * ATOMS + ATOMS, :] = values[
                    :, b * CHANNELS : b * CHANNELS + CHANNELS
                ]
        near = nbasis[pl.ds(q * 3, 3)].reshape(3 * BASES * ATOMS, CHANNELS)
        acc[0:ATOMS, :] += dot(rad[...], near)

    state = {"halo": halo_f}

    def hook1(step):
        if step == 0:
            arrive(state["halo"])
            state["halo"] = halo(1, 0, nfeat)
            message_block(jnp.int32(4))
        elif step == 1:
            arrive(state["halo"])
            state["halo"] = halo(2, 0, nfeat)
            state["more"] = halo(3, 0, nfeat)
            message_block(jnp.int32(3))
            message_block(jnp.int32(5))
        elif step == 2:
            arrive(state["halo"])
            message_block(jnp.int32(1))
            message_block(jnp.int32(7))
        else:
            last = halo(4, 0, nfeat)
            arrive(state["more"])
            message_block(jnp.int32(0))
            message_block(jnp.int32(6))
            arrive(last)
            message_block(jnp.int32(2))
            message_block(jnp.int32(8))

    def neutralise(value):
        row0 = jnp.broadcast_to(value[7:8, :], (8, 128))
        row1 = jnp.broadcast_to(value[15:16, :], (8, 128))
        total = jnp.where(lane8 < 8, pltpu.roll(row1, 120, axis=1), row0)
        total = jnp.where(lane8 < 64, total, pltpu.roll(total, 64, axis=1))
        count = jnp.sum(jnp.where(lane8 == 16, row1, 0.0), axis=1, keepdims=True)
        state["mean"] = (total / count)[0:1, :]
        parts = []
        for g in range(0, SUB, 8):
            tile = value[g : g + 8, :]
            live = jnp.broadcast_to(tile[7:8, :], (8, 128))
            live_c = jnp.sum(jnp.where(lane8 == row8, live, 0.0), axis=1, keepdims=True)
            live_s = jnp.sum(jnp.where(lane8 == row8 + 64, live, 0.0), axis=1, keepdims=True)
            parts.append(tile - jnp.where(lane8 < 64, live_c, live_s) * state["mean"])
        return jnp.concatenate(parts, axis=0)

    out_z = reduce_gather(
        0, tiles, part1, gotz1, mid1, goty1, low1, gotx1, up1, full1, neutralise, hook1
    )
    mean = state["mean"]

    pre_near = dot(acc[0:ATOMS, :].astype(BF16), wmix_ref[...])
    uv[:, CHANNELS : 2 * CHANNELS] = nbasis[13]

    prod[0:128, 0:256] = jnp.zeros((128, 256), F32)
    for d in range(EDGE):
        if d > 0:
            arrive([copies[d - 1] for copies in out_z])
        t = tile_at(EDGE - d)
        f_h, f_l = split(filt[t] * full1[t].astype(F32))
        fs_h[t] = f_h
        fs_l[t] = f_l
        prod[0:128, 0:256] += dot3(f_h, f_l, wave_h[t], wave_l[t], TN)

    potential = prod[0:64, 0:128] + prod[64:128, 128:256]
    pre = pre_near + dot(potential.astype(BF16), wlong_ref[...], TN)
    gate = sigmoid(pre)
    refined = own.astype(F32) + pre * gate
    outer = sigmoid(refined)
    readout = wenergy_ref[...]
    grad_new = live_col * readout * (outer * (1.0 + refined * (1.0 - outer)))
    grad_pre = (grad_new * (gate * (1.0 + pre * (1.0 - gate)))).astype(BF16)
    adjoint = dot(grad_pre, wmix_ref[...], NT).astype(BF16)
    nadj[13] = adjoint
    wlong2 = jnp.concatenate([wlong_ref[...], wlong_ref[...]], axis=0)
    pull_rows = dot(grad_pre, wlong2, NT)
    p_h, p_l = split(
        jnp.concatenate(
            [jnp.where(half, pull_rows, 0.0), jnp.where(half, 0.0, pull_rows)], axis=0
        )
    )

    tiles = []
    for d in (4, 3, 5, 2, 6, 1, 7, 0):
        t = tile_at(d)
        part2[t] = dot3(wave_h[t], wave_l[t], p_h, p_l).astype(BF16)
        if d > 0:
            tiles.append(send_tile(1, part2, gotz2, d))
    state["halo"] = halo(0, 1, nadj)

    upd_ref[...] = refined.astype(BF16)
    energy_col = jnp.sum(refined * outer * readout, axis=1, keepdims=True)
    energy_ref[...] = (
        jnp.transpose(jnp.broadcast_to(energy_col, (ATOMS, ATOMS)))[0:1, :] * live_row
    )

    first = iota((ATOMS, ATOMS), 0) < 64
    pull_t = jnp.transpose(pull_rows)
    neutral_t = jnp.transpose((charge - mean) * live_col)
    pull[0:128, 0:128] = jnp.where(first, 0.0, pull_t)
    pull[0:128, 128:256] = jnp.where(first, pull_t, 0.0)
    pull[128:256, 0:128] = jnp.where(first, 0.0, neutral_t)
    pull[128:256, 128:256] = jnp.where(first, neutral_t, 0.0)

    for b in range(BASES):
        uv[b * ATOMS : b * ATOMS + ATOMS, 0:CHANNELS] = adjoint
    for axis in range(3):
        acc[axis * ATOMS : axis * ATOMS + ATOMS, :] = jnp.zeros((ATOMS, ATOMS), F32)

    def force_block(q):
        for oz in range(3):
            for b in range(BASES):
                rows = slice(b * ATOMS, b * ATOMS + ATOMS)
                near = jnp.concatenate([nbasis[q * 3 + oz, rows, :], nadj[q * 3 + oz]], axis=1)
                prod[rows, oz * 128 : oz * 128 + 128] = dot(uv[rows, :], near, NT)
        for row0 in range(0, ATOMS, STRIP):
            total_x = total_y = total_z = None
            for oz in range(3):
                dx, dy, dz, base, decay = pair(q, oz, row0, STRIP)
                envelope = base * base
                double = base + base
                strength = None
                for b, rate in enumerate((1.0, 3.0, 8.0, 20.0)):
                    got = prod[
                        b * ATOMS + row0 : b * ATOMS + row0 + STRIP, oz * 128 : oz * 128 + 128
                    ]
                    term = decay[b] * (envelope * rate + double) * got
                    strength = term if strength is None else strength + term
                if total_x is None:
                    total_x, total_y, total_z = strength * dx, strength * dy, strength * dz
                else:
                    total_x = total_x + strength * dx
                    total_y = total_y + strength * dy
                    total_z = total_z + strength * dz
            acc[row0 : row0 + STRIP, :] += total_x
            acc[128 + row0 : 128 + row0 + STRIP, :] += total_y
            acc[256 + row0 : 256 + row0 + STRIP, :] += total_z

    def hook2(step):
        if step != 3:
            drain()
        if step == 0:
            arrive(state["halo"])
            state["halo"] = halo(1, 1, nadj)
            force_block(jnp.int32(4))
        elif step == 1:
            arrive(state["halo"])
            state["halo"] = halo(2, 1, nadj)
            state["more"] = halo(3, 1, nadj)
            force_block(jnp.int32(3))
            force_block(jnp.int32(5))
        elif step == 2:
            arrive(state["halo"])
            force_block(jnp.int32(1))
            force_block(jnp.int32(7))
        else:
            last = halo(4, 1, nadj)
            arrive(state["more"])
            force_block(jnp.int32(0))
            force_block(jnp.int32(6))
            arrive(last)
            force_block(jnp.int32(2))
            force_block(jnp.int32(8))

    out_z = reduce_gather(
        1, tiles, part2, gotz2, mid2, goty2, low2, gotx2, up2, full2, lambda v: v, hook2
    )

    lane = iota((ATOMS, ATOMS), 1)
    columns = jnp.zeros((ATOMS, ATOMS), F32)
    for axis in range(3):
        near_sum = jnp.sum(acc[axis * ATOMS : axis * ATOMS + ATOMS, :], axis=1, keepdims=True)
        columns = jnp.where(lane == axis, near_sum, columns)
    near_force = jnp.transpose(columns)[0:8, :] * (-2.0 / CUTOFF2)
    r_h, r_l = split(pull[...])

    prod[0:8, 0:128] = jnp.zeros((8, 128), F32)
    for d in range(EDGE):
        if d > 0:
            arrive([copies[d - 1] for copies in out_z])
        t = tile_at(EDGE - d)
        b_h, b_l = split(filt[t] * full2[t].astype(F32))
        left_h = jnp.concatenate([fs_h[t], b_h], axis=1)
        left_l = jnp.concatenate([fs_l[t], b_l], axis=1)
        mixed = dot3(left_h, left_l, r_h, r_l)
        waves = wave_f[t]
        d_h, d_l = split(
            waves[:, 0:128] * mixed[:, 0:128] - waves[:, 128:256] * mixed[:, 128:256]
        )
        index = iota((8, ROWS), 1) + t * ROWS
        axis_row = iota((8, ROWS), 0)
        group = lax.shift_right_logical(index, 3)
        group_x = lax.shift_right_logical(group * 79, 10)
        value_x = group_x - TOP
        value_y = group - group_x * SIDE - TOP
        value_z = lax.bitwise_and(index, 7)
        values = jnp.where(axis_row == 0, value_x, jnp.where(axis_row == 1, value_y, value_z))
        rows = values.astype(F32).astype(BF16)
        prod[0:8, 0:128] += dot(rows, d_h) + dot(rows, d_l)

    force = near_force - prod[0:8, 0:128] * (2.0 * math.pi / EDGE)
    for axis in range(3):
        force_ref[axis] = force[axis : axis + 1, :]
    drain()


def shards(
    features,
    positions,
    counts,
    w_proj,
    w_mix,
    w_long,
    w_charge,
    charge_bias,
    w_energy,
    k_filter,
    k_index,
):
    hbm = pl.BlockSpec(memory_space=pltpu.HBM)
    vmem = pl.BlockSpec(memory_space=pltpu.VMEM)
    dma = pltpu.SemaphoreType.DMA
    reduce_buffers = [
        pltpu.VMEM((TILES, ROWS, 128), BF16),
        pltpu.VMEM((EDGE - 1, ROWS, 128), BF16),
        pltpu.VMEM((PIECES, EDGE, SUB, 128), F32),
        pltpu.VMEM((EDGE - 1, PIECES, SUB, 128), F32),
        pltpu.VMEM((PIECES, SUB, 128), F32),
        pltpu.VMEM((EDGE - 1, PIECES, SUB, 128), F32),
        pltpu.VMEM((PIECES, EDGE, SUB, 128), BF16),
        pltpu.VMEM((TILES, ROWS, 128), BF16),
    ]
    updated, energy, force = pl.pallas_call(
        block_kernel,
        name="block",
        out_shape=(
            jax.ShapeDtypeStruct((ATOMS, CHANNELS), BF16),
            jax.ShapeDtypeStruct((1, ATOMS), F32),
            jax.ShapeDtypeStruct((3, 1, ATOMS), F32),
        ),
        in_specs=[pl.BlockSpec(memory_space=pltpu.SMEM)] + [hbm] * 10,
        out_specs=(vmem, vmem, vmem),
        scratch_shapes=[
            pltpu.VMEM((ATOMS, CHANNELS), BF16),
            pltpu.VMEM((3, 1, ATOMS), F32),
            pltpu.VMEM((BASES, CHANNELS, CHANNELS), BF16),
            pltpu.VMEM((CHANNELS, CHANNELS), BF16),
            pltpu.VMEM((64, CHANNELS), BF16),
            pltpu.VMEM((64, CHANNELS), BF16),
            pltpu.VMEM((1, 64), F32),
            pltpu.VMEM((1, CHANNELS), F32),
            pltpu.VMEM((64, WAVES), F32),
            pltpu.VMEM((3, WAVES), jnp.int32),
            pltpu.VMEM((27, ATOMS + 16, CHANNELS), BF16),
            pltpu.VMEM((27, ATOMS, CHANNELS), BF16),
            pltpu.VMEM((16, ATOMS), F32),
            pltpu.VMEM((6, 8, ATOMS), F32),
            pltpu.VMEM((8, 128), F32),
            pltpu.VMEM((TILES, ROWS, 256), F32),
            pltpu.VMEM((TILES, ROWS, 256), BF16),
            pltpu.VMEM((TILES, ROWS, 256), BF16),
            pltpu.VMEM((TILES, ROWS, 128), F32),
            pltpu.VMEM((TILES, ROWS, 128), BF16),
            pltpu.VMEM((TILES, ROWS, 128), BF16),
        ]
        + reduce_buffers
        + reduce_buffers
        + [
            pltpu.VMEM((3, ATOMS, ATOMS), F32),
            pltpu.VMEM((ATOMS, 3 * BASES * ATOMS), BF16),
            pltpu.VMEM((CHANNELS, BASES * CHANNELS), BF16),
            pltpu.VMEM((27, BASES * ATOMS, CHANNELS), BF16),
            pltpu.VMEM((BASES * ATOMS, CHANNELS), F32),
            pltpu.VMEM((BASES * ATOMS, 3 * 128), F32),
            pltpu.VMEM((BASES * ATOMS, 2 * CHANNELS), BF16),
            pltpu.VMEM((256, 256), F32),
            dma((10,)),
            dma((2, 5, PIECES, EDGE - 1)),
            dma((2, 5, PIECES, EDGE - 1)),
            dma((2, 5, 2)),
            dma((2, 5, 2)),
        ],
        compiler_params=pltpu.CompilerParams(
            collective_id=0, has_side_effects=True, vmem_limit_bytes=67043328
        ),
    )(
        counts.reshape(1),
        features[0, 0, 0],
        positions.reshape(3, 1, ATOMS),
        w_proj,
        w_mix,
        w_long,
        w_charge,
        charge_bias.reshape(1, 64),
        w_energy.reshape(1, CHANNELS),
        k_filter,
        k_index,
    )
    return (
        updated[None, None, None],
        energy.reshape(1, 1, 1, ATOMS),
        force.reshape(1, 1, 1, 3, ATOMS),
    )


def solution(mesh):
    cells = P("gx", "gy", "gz")
    in_specs = (cells, cells, cells) + (P(),) * 8
    return jax.shard_map(
        shards, mesh=mesh, in_specs=in_specs, out_specs=(cells, cells, cells), check_vma=False
    )
```

time: 99 us -> 82.4 us (0.83)
  Pallas kernels: 88.3 us -> 78.3 us
  local copies, waits for them, and re-layouts: 7.31 us -> 2.61 us
  other arithmetic: 1.47 us -> 0 us
    pallas_call x1, Pallas kernels: 88.3 us -> 78.3 us  [shards(): pl.pallas_call(block_kernel, name='block', out_shape=(jax.ShapeDtypeStruc...]
    unnamed x18 -> x7, local copies, waits for them, and re-layouts: 7.31 us -> 2.61 us
    another operation x2 -> x0, other arithmetic: 1.47 us -> none  [shards(): rows = jnp.stack([jnp.concatenate([charge_bias, charge_bias]), w_energy])]
where the time goes in v2:
time: 82.4 us; the launch traced here: 82.2 us
  Pallas kernels  78.3 us (95%)
  local copies, waits for them, and re-layouts  2.61 us (3%)
  between operations  1.3 us (2%)
    pallas_call x1, Pallas kernels, shards(): pl.pallas_call(block_kernel, name='block', out_shape=(jax.ShapeDtypeStruc...  78.3 us
    unnamed x7, local copies, waits for them, and re-layouts  2.61 us

profile of v2, /device:TPU:1, one launch (start us, length us, event | category | flops | bytes accessed | tf_op | source)
XLA Modules:
  0.0 82.2 jit_solution(17037526995042723855)
XLA Ops:
  1.3 78.3 %block.1 = (bf16[128,128]{1,0:T(8,128)(2,1)}, f32[1,128]{1,0:T(1,128)}, f32[3,1,128]{2,1,0:T(1,128)}) custom-call(s32[1]{0:T(128)} %bitcast.10.counts_ref, bf16[128,128]{1,0:T(8,128)(2,1)} %bitcast.11, f32[3,1,128]{2,1,0:T(1,128)} %bitcast.13, bf16[4,128,128]{2,1,0:T(8,128)(2,1)} %wproj_hbm.1, bf16[128,128]{1,0:T(8,128)(2,1)} %wmix_hbm.1, ...), custom_call_target="tpu_custom_call" | custom-call | tf_op jit(solution)/shard_map/block/pallas_call | solution.py:704
  79.6 0.0 copy-start.1
  79.6 1.4 %copy.19 = bf16[1,1,1,128,128]{4,3,2,1,0:T(8,128)(2,1)} copy(bf16[1,1,1,128,128]{4,3,2,1,0:T(8,128)(2,1)} %bitcast.12) | data formatting | bytes 65536
  80.9 0.0 copy-done.1
  80.9 0.0 copy-start
  80.9 0.5 copy.20
  81.5 0.2 copy-done
  81.6 0.6 copy.21
Async XLA Ops:
  79.6 1.4 %copy-start.1 = (f32[1,128]{1,0:T(1,128)S(1)}, f32[1,128]{1,0:T(1,128)}, u32[]{:S(2)}) copy-start(f32[1,128]{1,0:T(1,128)} %get-tuple-element.7) | copy-start | bytes 1540
  80.9 0.7 copy-start

commit v3 on v2

--- a/solution.py
+++ b/solution.py
@@ -18,9 +18,10 @@
 TOP = 6
 SIDE = 2 * TOP + 1
 TILES = 8
-ROWS = 192
+ROWS = 176
+GROUPS = 22
 PIECES = 1
-PIECE = 192
+PIECE = 176
 SUB = 24
 SLOTS = TILES * ROWS
 F32 = jnp.float32
@@ -236,7 +237,11 @@
             for d in range(1, EDGE):
                 value = value + gotz[d - 1, rows, :].astype(F32)
             for c in range(EDGE):
-                mid[p, c] = value[c * SUB : c * SUB + SUB, :]
+                rows = value[c * SUB : min(c * SUB + SUB, PIECE), :]
+                short = SUB - rows.shape[0]
+                if short:
+                    rows = jnp.concatenate([rows, jnp.zeros((short, 128), F32)], axis=0)
+                mid[p, c] = rows.astype(mid.dtype)
             stages.append(
                 spread(
                     1, (kind, 1, p), lambda peer: mid.at[p, peer], lambda s: goty.at[s, p]
@@ -246,10 +251,10 @@
         copies, stages = stages, []
         for p in range(PIECES):
             arrive(copies[p])
-            value = mid[p, place[1]]
+            value = mid[p, place[1]].astype(F32)
             for d in range(1, EDGE):
-                value = value + goty[d - 1, p]
-            low[p] = value
+                value = value + goty[d - 1, p].astype(F32)
+            low[p] = value.astype(low.dtype)
             stages.append(
                 spread(0, (kind, 2, p), lambda peer: low.at[p], lambda s: gotx.at[s, p])
             )
@@ -257,9 +262,9 @@
         copies, stages = stages, []
         for p in range(PIECES):
             arrive(copies[p])
-            value = low[p]
+            value = low[p].astype(F32)
             for d in range(1, EDGE):
-                value = value + gotx[d - 1, p]
+                value = value + gotx[d - 1, p].astype(F32)
             up[p, place[1]] = finish(value).astype(BF16)
             stages.append(
                 spread(
@@ -272,7 +277,11 @@
             arrive(copies[p])
             rows = pl.ds(p * PIECE, PIECE)
             full[place[2], p * PIECE : p * PIECE + PIECE, :] = jnp.concatenate(
-                [up[p, c].astype(F32) for c in range(EDGE)], axis=0
+                [
+                    up[p, c, 0 : min(SUB, PIECE - c * SUB), :].astype(F32)
+                    for c in range(EDGE)
+                ],
+                axis=0,
             ).astype(BF16)
             stages.append(
                 spread(
@@ -316,8 +325,14 @@
     wcharge2 = jnp.concatenate([wcharge_ref[...], wcharge_ref[...]], axis=0)
     row[0:1, 0:64] = bias_ref[...]
     bias = row[...]
-    charge_pre = dot(masked, wcharge2, NT) + (bias + pltpu.roll(bias, 64, axis=1))[0:1, :]
-    charge = charge_pre * sigmoid(charge_pre) * live_col
+    bias_row = (bias + pltpu.roll(bias, 64, axis=1))[0:1, :]
+    charge_pre = dot(masked, wcharge2, NT) + bias_row
+    squares = wcharge2.astype(F32) * wcharge2.astype(F32)
+    reach = jnp.sqrt(3.0 * dot(jnp.ones((8, CHANNELS), BF16), squares.astype(BF16), NT)[0:1, :])
+    guess = bias_row * sigmoid(bias_row) * (2.0 / 3.0)
+    for side in (bias_row + reach, bias_row - reach):
+        guess = guess + side * sigmoid(side) * (1.0 / 6.0)
+    charge = (charge_pre * sigmoid(charge_pre) - guess) * live_col
     own_total = jnp.broadcast_to(jnp.sum(charge, axis=0, keepdims=True), (8, 128))
     own_count = jnp.broadcast_to(jnp.sum(live_col, axis=0, keepdims=True), (8, 128))
     z_c = trig[4]
@@ -326,7 +341,7 @@
     y_s = [jnp.broadcast_to(trig[3, m : m + 1, :], (8, ATOMS)) for m in range(TOP + 1)]
 
     def put_wave(group, c, s):
-        tile, row = group // 24, (group % 24) * 8
+        tile, row = group // GROUPS, (group % GROUPS) * 8
         wave_f[tile, row : row + 8, 0:ATOMS] = c
         wave_f[tile, row : row + 8, ATOMS : 2 * ATOMS] = s
 
@@ -365,7 +380,6 @@
     both_l = jnp.concatenate([q_l, l_l], axis=1)
     spare = lax.rem(iota((ROWS, 128), 0), 8) == 7
 
-    pl.semaphore_wait(barrier, 3 * (EDGE - 1) + 4)
 
     def shift(axis, stage, kind, buffer, source, before, after, width):
         ring = []
@@ -391,25 +405,38 @@
         column = (1, 0, 2)[stage - 2] * 3
         return shift(1, stage, kind, buffer, 9 + column, column, 18 + column, 3)
 
-    halo_f = halo(0, 0, nfeat)
     lane8 = iota((8, 128), 1)
     row8 = iota((8, 128), 0)
-    moved = jnp.where(lane8 == 16, own_count, pltpu.roll(own_total, 8, axis=1))
-    lanes = iota((ROWS, 128), 1)
-    member = lax.rem(iota((ROWS, 128), 0), 24) // 8
-    first_free = (member == 0) & (lanes >= 8) & (lanes < 64)
-    second_free = (member == 1) & (lanes >= 8) & (lanes <= 16)
-    extra = jnp.where(first_free, own_total[0:1, :], jnp.where(second_free, moved[0:1, :], 0.0))
+    moved = pltpu.roll(own_total, 8, axis=1)
+    extra = jnp.where(
+        lane8 < 8,
+        0.0,
+        jnp.where(
+            lane8 < 64,
+            own_total,
+            jnp.where(
+                lane8 < 72,
+                0.0,
+                jnp.where(lane8 < 80, moved, jnp.where(lane8 == 80, own_count, 0.0)),
+            ),
+        ),
+    )[0:1, :]
     tiles = []
-    for d in (4, 3, 5, 2, 6, 1, 7, 0):
+    order = (4, 3, 5, 2, 6, 1, 7, 0)
+    for step, d in enumerate(order):
         t = tile_at(d)
         w_h, w_l = split(wave_f[t])
         wave_h[t] = w_h
         wave_l[t] = w_l
         sums = dot3(w_h, w_l, both_h, both_l)
         part1[t] = jnp.where(spare, sums[:, 128:256] + extra, sums[:, 0:128]).astype(BF16)
-        if d > 0:
+        if step == len(order) // 2 - 1:
+            pl.semaphore_wait(barrier, 3 * (EDGE - 1) + 4)
+            for early in order[:step]:
+                tiles.append(send_tile(0, part1, gotz1, early))
+        if step >= len(order) // 2 - 1 and d > 0:
             tiles.append(send_tile(0, part1, gotz1, d))
+    halo_f = halo(0, 0, nfeat)
 
     for load in loads[4:]:
         load.wait()
@@ -501,10 +528,9 @@
 
     def neutralise(value):
         row0 = jnp.broadcast_to(value[7:8, :], (8, 128))
-        row1 = jnp.broadcast_to(value[15:16, :], (8, 128))
-        total = jnp.where(lane8 < 8, pltpu.roll(row1, 120, axis=1), row0)
+        total = jnp.where(lane8 < 8, pltpu.roll(row0, 56, axis=1), row0)
         total = jnp.where(lane8 < 64, total, pltpu.roll(total, 64, axis=1))
-        count = jnp.sum(jnp.where(lane8 == 16, row1, 0.0), axis=1, keepdims=True)
+        count = jnp.sum(jnp.where(lane8 == 80, row0, 0.0), axis=1, keepdims=True)
         state["mean"] = (total / count)[0:1, :]
         parts = []
         for g in range(0, SUB, 8):
@@ -691,16 +717,18 @@
     hbm = pl.BlockSpec(memory_space=pltpu.HBM)
     vmem = pl.BlockSpec(memory_space=pltpu.VMEM)
     dma = pltpu.SemaphoreType.DMA
-    reduce_buffers = [
-        pltpu.VMEM((TILES, ROWS, 128), BF16),
-        pltpu.VMEM((EDGE - 1, ROWS, 128), BF16),
-        pltpu.VMEM((PIECES, EDGE, SUB, 128), F32),
-        pltpu.VMEM((EDGE - 1, PIECES, SUB, 128), F32),
-        pltpu.VMEM((PIECES, SUB, 128), F32),
-        pltpu.VMEM((EDGE - 1, PIECES, SUB, 128), F32),
-        pltpu.VMEM((PIECES, EDGE, SUB, 128), BF16),
-        pltpu.VMEM((TILES, ROWS, 128), BF16),
-    ]
+    def reduce_buffers(narrow_y, narrow_z):
+        return [
+            pltpu.VMEM((TILES, ROWS, 128), BF16),
+            pltpu.VMEM((EDGE - 1, ROWS, 128), BF16),
+            pltpu.VMEM((PIECES, EDGE, SUB, 128), narrow_y),
+            pltpu.VMEM((EDGE - 1, PIECES, SUB, 128), narrow_y),
+            pltpu.VMEM((PIECES, SUB, 128), narrow_z),
+            pltpu.VMEM((EDGE - 1, PIECES, SUB, 128), narrow_z),
+            pltpu.VMEM((PIECES, EDGE, SUB, 128), BF16),
+            pltpu.VMEM((TILES, ROWS, 128), BF16),
+        ]
+
     updated, energy, force = pl.pallas_call(
         block_kernel,
         name="block",
@@ -734,8 +762,8 @@
             pltpu.VMEM((TILES, ROWS, 128), BF16),
             pltpu.VMEM((TILES, ROWS, 128), BF16),
         ]
-        + reduce_buffers
-        + reduce_buffers
+        + reduce_buffers(BF16, F32)
+        + reduce_buffers(BF16, BF16)
         + [
             pltpu.VMEM((3, ATOMS, ATOMS), F32),
             pltpu.VMEM((ATOMS, 3 * BASES * ATOMS), BF16),
@@ -752,20 +780,20 @@
             dma((2, 5, 2)),
         ],
         compiler_params=pltpu.CompilerParams(
-            collective_id=0, has_side_effects=True, vmem_limit_bytes=67043328
+            collective_id=0, has_side_effects=True, vmem_limit_bytes=48 * 1024 * 1024
         ),
     )(
         counts.reshape(1),
-        features[0, 0, 0],
-        positions.reshape(3, 1, ATOMS),
-        w_proj,
-        w_mix,
-        w_long,
-        w_charge,
-        charge_bias.reshape(1, 64),
-        w_energy.reshape(1, CHANNELS),
-        k_filter,
-        k_index,
+        pltpu.with_memory_space_constraint(features[0, 0, 0], pltpu.HBM),
+        pltpu.with_memory_space_constraint(positions.reshape(3, 1, ATOMS), pltpu.HBM),
+        pltpu.with_memory_space_constraint(w_proj, pltpu.HBM),
+        pltpu.with_memory_space_constraint(w_mix, pltpu.HBM),
+        pltpu.with_memory_space_constraint(w_long, pltpu.HBM),
+        pltpu.with_memory_space_constraint(w_charge, pltpu.HBM),
+        pltpu.with_memory_space_constraint(charge_bias.reshape(1, 64), pltpu.HBM),
+        pltpu.with_memory_space_constraint(w_energy.reshape(1, CHANNELS), pltpu.HBM),
+        pltpu.with_memory_space_constraint(k_filter, pltpu.HBM),
+        pltpu.with_memory_space_constraint(k_index, pltpu.HBM),
     )
     return (
         updated[None, None, None],

time: 82.4 us -> 78 us (0.947)
  Pallas kernels: 78.3 us -> 74.8 us
  local copies, waits for them, and re-layouts: 2.61 us -> 1.69 us
    pallas_call x1, Pallas kernels: 78.3 us -> 74.8 us  [shards(): pl.pallas_call(block_kernel, name='block', out_shape=(jax.ShapeDtypeStruc...]
    unnamed x7 -> x3, local copies, waits for them, and re-layouts: 2.61 us -> 1.69 us
where the time goes in v3:
time: 78 us; the launch traced here: 77.8 us
  Pallas kernels  74.8 us (96%)
  local copies, waits for them, and re-layouts  1.69 us (2%)
  between operations  1.29 us (2%)
    pallas_call x1, Pallas kernels, shards(): pl.pallas_call(block_kernel, name='block', out_shape=(jax.ShapeDtypeStruc...  74.8 us
    unnamed x3, local copies, waits for them, and re-layouts  1.69 us

profile of v3, /device:TPU:1, one launch (start us, length us, event | category | flops | bytes accessed | tf_op | source)
XLA Modules:
  0.0 77.8 jit_solution(13194287887289155379)
XLA Ops:
  1.3 74.8 %block.1 = (bf16[128,128]{1,0:T(8,128)(2,1)S(1)}, f32[1,128]{1,0:T(1,128)S(1)}, f32[3,1,128]{2,1,0:T(1,128)S(1)}) custom-call(s32[1]{0:T(128)} %bitcast.10.counts_ref, bf16[128,128]{1,0:T(8,128)(2,1)} %bitcast.14, f32[3,1,128]{2,1,0:T(1,128)} %bitcast.15, bf16[4,128,128]{2,1,0:T(8,128)(2,1)} %wproj_hbm.1, bf16[128,128]{1,0:T(8,128)(2,1)} %wmix_hbm.1, ...), custom_call_target="tpu_custom_call" | custom-call | tf_op jit(solution)/shard_map/block/pallas_call | solution.py:732
  76.1 0.6 copy.19
  76.7 0.5 copy.20
  77.2 0.6 copy.21

commit v4 on v3

--- a/solution.py
+++ b/solution.py
@@ -762,7 +762,7 @@
             pltpu.VMEM((TILES, ROWS, 128), BF16),
             pltpu.VMEM((TILES, ROWS, 128), BF16),
         ]
-        + reduce_buffers(BF16, F32)
+        + reduce_buffers(BF16, BF16)
         + reduce_buffers(BF16, BF16)
         + [
             pltpu.VMEM((3, ATOMS, ATOMS), F32),

time: 78 us -> 77.6 us (level)
  no operation moved by 1% of the time
where the time goes in v4:
time: 77.6 us; the launch traced here: 77.5 us
  Pallas kernels  74.5 us (96%)
  local copies, waits for them, and re-layouts  1.69 us (2%)
  between operations  1.29 us (2%)
    pallas_call x1, Pallas kernels, shards(): pl.pallas_call(block_kernel, name='block', out_shape=(jax.ShapeDtypeStruc...  74.5 us
    unnamed x3, local copies, waits for them, and re-layouts  1.69 us

profile of v4, /device:TPU:1, one launch (start us, length us, event | category | flops | bytes accessed | tf_op | source)
XLA Modules:
  0.0 77.5 jit_solution(9647451288294528931)
XLA Ops:
  1.3 74.5 %block.1 = (bf16[128,128]{1,0:T(8,128)(2,1)S(1)}, f32[1,128]{1,0:T(1,128)S(1)}, f32[3,1,128]{2,1,0:T(1,128)S(1)}) custom-call(s32[1]{0:T(128)} %bitcast.10.counts_ref, bf16[128,128]{1,0:T(8,128)(2,1)} %bitcast.14, f32[3,1,128]{2,1,0:T(1,128)} %bitcast.15, bf16[4,128,128]{2,1,0:T(8,128)(2,1)} %wproj_hbm.1, bf16[128,128]{1,0:T(8,128)(2,1)} %wmix_hbm.1, ...), custom_call_target="tpu_custom_call" | custom-call | tf_op jit(solution)/shard_map/block/pallas_call | solution.py:732
  75.8 0.6 copy.19
  76.4 0.5 copy.20
  76.9 0.6 copy.21
